TPU v7x, 512 devices: a whole 4x8x8 slice. The times are simulated.
512 devices in a mesh: node: 16 (over y, core), tile: 32 (over z, x).
Axes of the slice: x: 4, y: 8, z: 8, core: 2. Of those that a mesh axis runs over, the one named last changes fastest.
Arguments:
- child_cost: float32 [128, 1024, 1024], P('node', 'tile'), as said below
- child_weight: int32 [128], P('node'), may hold values from 1 to 16
- parent_of: int32 [128], P('node'), may hold values from 0 to 31, as said below
- dyn_a: bfloat16 [1024, 1024], replicated, may hold values from -0.1875 to 0.1875
- dyn_b: bfloat16 [1024, 256], replicated, may hold values from -0.1875 to 0.1875
- state_weight: float32 [32, 1024], P('node', 'tile'), may hold values from 0.2 to 5
- input_weight: float32 [32, 256], P('node'), may hold values from 0.3 to 3
- parent_cov: bfloat16 [32, 1024, 1024], P('node', 'tile'), as said below
- noise_cov: float32 [128, 1024], P('node', 'tile'), may hold values from 0.05 to 1
Outputs:
- parent_cost: float32 [32, 1024, 1024], P('node', 'tile')
- parent_gain: float32 [32, 256, 1024], P('node', 'tile')
- child_cov: float32 [128, 1024, 1024], P('node', 'tile')
Inputs may be any that keep to these rules, and one draw needn't show every extreme that they name: `parent_of`: the 128 children are listed by parent: the numbers never fall; every parent has 2 to 8 children, some parent exactly 8 and some exactly 2; parents 4k to 4k + 3 together have exactly 16 children. `child_cost`: each matrix is symmetric positive definite. `parent_cov`: each matrix is symmetric positive definite.
All inputs are finite; a program needn't handle non-finite values.
Results may differ from a plain program's by a relative error of at most 0.0022.
Values may be sent and summed in bfloat16 or wider, within the bound.
A program may use at most 64 MiB of HBM per device.

v0:
```python
import functools

import jax
import jax.numpy as jnp
from jax import lax
from jax.experimental import pallas as pl
from jax.experimental.pallas import tpu as pltpu
from jax.sharding import PartitionSpec as P

F32, BF16 = jnp.float32, jnp.bfloat16
MESH = pl.DeviceIdType.MESH


def split(v):
    high = v.astype(BF16)
    return high, (v - high.astype(F32)).astype(BF16)


def mm(a, b, dims=((1,), (0,))):
    return lax.dot_general(a, b, (dims, ((), ())), preferred_element_type=F32)


def mm2(a, b, dims=((1,), (0,))):
    return mm(a[0], b, dims) + mm(a[1], b, dims)


def mm3(a, b, dims=((1,), (0,))):
    return mm(a[0], b[0], dims) + (mm(a[0], b[1], dims) + mm(a[1], b[0], dims))


def total(terms):
    while len(terms) > 1:
        terms = [
            terms[i] + terms[i + 1] if i + 1 < len(terms) else terms[i]
            for i in range(0, len(terms), 2)
        ]
    return terms[0]


def small_inverse(d):
    b = len(d)
    if b == 2:
        r = 1.0 / (d[0][0] * d[1][1] - d[0][1] * d[0][1])
        off = -d[0][1] * r
        return [[d[1][1] * r, off], [off, d[0][0] * r]]
    h = b // 2
    span = range(h)
    x = small_inverse([[d[i][j] for j in span] for i in span])
    y = [[d[i][h + j] for j in span] for i in span]
    w = [[total([x[i][k] * y[k][j] for k in span]) for j in span] for i in span]
    s = [[None] * h for _ in span]
    for i in span:
        for j in range(i, h):
            s[i][j] = s[j][i] = d[h + i][h + j] - total([y[k][i] * w[k][j] for k in span])
    q = small_inverse(s)
    wq = [[total([w[i][k] * q[k][j] for k in span]) for j in span] for i in span]
    out = [[None] * b for _ in range(b)]
    for i in span:
        for j in range(i, h):
            out[i][j] = out[j][i] = x[i][j] + total([wq[i][k] * w[j][k] for k in span])
        for j in span:
            out[i][h + j] = out[h + j][i] = -wq[i][j]
            out[h + i][h + j] = q[i][j]
    return out


def sweep(a, trips, b=4, unroll=8):
    n = a.shape[0]
    lane = lax.broadcasted_iota(jnp.int32, (1, n), 1)
    lanes = lax.broadcasted_iota(jnp.int32, (n, n), 1)
    sub = lax.broadcasted_iota(jnp.int32, (n, 1), 0)

    def body(_, a):
        for low in range(0, unroll, b):
            ks = range(low, low + b)
            d = [[jnp.broadcast_to(a[i : i + 1, j : j + 1], (1, n)) for j in ks] for i in ks]
            inv = small_inverse(d)
            rows = [a[j : j + 1, :] for j in ks]
            in_rows = (sub >= low) & (sub < low + b)
            cols = [jnp.where(sub == k, -1.0, jnp.where(in_rows, 0.0, a[:, k : k + 1])) for k in ks]
            new = []
            for i in range(b):
                t = total([inv[i][j] * rows[j] for j in range(b)])
                for j in range(b):
                    t = jnp.where(lane == low + j, inv[i][j], t)
                new.append(t)
            a = jnp.where(((lanes >= low) & (lanes < low + b)) | in_rows, 0.0, a)
            for i in range(b):
                a = a - cols[i] * new[i]
        a = jnp.concatenate([a[unroll:], a[:unroll]], axis=0)
        return pltpu.roll(a, n - unroll, 1)

    return lax.fori_loop(0, trips, body, a)


HOPS = ((4, 3), (3, 4))


def kernel(
    cc, cw, po, a_in, b_in, sw, iw, pcov, nz,
    pc_out, pg_out, ch_out,
    ccv, a5, b5, at5, lt, e5, p5, acc, mine, theirs, wt, wr, iwr, eb,
    bh, bl, cpl, gv, gh, gl, pcv, pcr, pgr, spv, spr, chv,
    load_sem, loc_sem, out_sem, sa_s, sa_r, sb_s, sb_r, pa_s, pa_r,
    er_s, er_r, ef_s, ef_r, pr_s, pr_r, pf_s, pf_r,
    gs_s, gs_r, cs_s, cs_r, ss_s, ss_r, sf_s, sf_r,
):
    n, t = lax.axis_index("node"), lax.axis_index("tile")
    c, y = lax.rem(n, 2), n // 2
    z, x = t // 4, lax.rem(t, 4)
    oc = 1 - c
    own, jq = x // 2, lax.rem(x, 2)

    def dev(core, zz, xx):
        return (2 * y + core, 4 * zz + xx)

    def xs(dx):
        return lax.rem(x + dx + 4, 4)

    def zs(dz):
        return lax.rem(z + dz + 8, 8)

    def remote(src, dst, ssem, rsem, where):
        return pltpu.make_async_remote_copy(
            src_ref=src, dst_ref=dst, send_sem=ssem, recv_sem=rsem,
            device_id=where, device_id_type=MESH,
        )

    zlane = pl.multiple_of(z * 128, 128)

    barrier = pltpu.get_barrier_semaphore()
    for dx in range(4):
        for core in ((oc,) if dx == 0 else (c, oc)):
            pl.semaphore_signal(barrier, inc=1, device_id=dev(core, z, xs(dx)), device_id_type=MESH)
    for dz in (1, -1):
        pl.semaphore_signal(barrier, inc=1, device_id=dev(c, zs(dz), x), device_id_type=MESH)

    loads = [
        pltpu.make_async_copy(cc, ccv, load_sem.at[0]),
        pltpu.make_async_copy(b_in, b5, load_sem.at[1]),
        pltpu.make_async_copy(a_in, a5, load_sem.at[2]),
    ]
    for cp in loads:
        cp.start()

    first = 4 * y
    coef = [
        [jnp.where(po[k] == first + q, cw[k].astype(F32), 0.0) for q in range(4)]
        for k in range(8)
    ]
    sub8 = lax.broadcasted_iota(jnp.int32, (8, 128), 0)
    tile = jnp.zeros((8, 128), F32)
    for q in range(4):
        s = total([coef[k][q] for k in range(8)])
        tile = jnp.where(sub8 == q, s, tile)
    wt[...] = tile

    loads[0].wait()

    def weigh(i, _):
        cols = pl.ds(pl.multiple_of(i * 256, 256), 256)
        for h in range(2):
            sums = [None] * 4
            for k in range(8):
                v = ccv[k, 16 * h : 16 * h + 16, cols]
                for q in range(4):
                    term = coef[k][q] * v
                    sums[q] = term if k == 0 else sums[q] + term
            for q in range(4):
                mine[q, h, :, cols] = sums[q]
        return 0

    lax.fori_loop(0, 4, weigh, 0)

    pl.semaphore_wait(barrier, 9)

    pair = dev(oc, z, x)
    swap = [
        remote(mine.at[:, oc], theirs, sa_s.at[0], sa_r.at[0], pair),
        remote(wt, wr, sa_s.at[1], sa_r.at[1], pair),
        remote(iw, iwr, sa_s.at[2], sa_r.at[2], pair),
    ]
    for cp in swap:
        cp.start()

    def cov_copy(dx, other):
        q = xs(dx)
        core = oc if other else c
        return remote(
            pcov.at[lax.rem(q, 2), pl.ds(pl.multiple_of(16 * core, 16), 16)],
            p5.at[z, x, core], pa_s.at[dx, int(other)], pa_r.at[dx], dev(core, z, q),
        )

    def cov_local():
        return pltpu.make_async_copy(
            pcov.at[jq, pl.ds(pl.multiple_of(16 * c, 16), 16)], p5.at[z, x, c], loc_sem.at[0]
        )

    for dx in (2, 1, 3, 0):
        @pl.when(xs(dx) // 2 == c)
        def _(dx=dx):
            cov_copy(dx, True).start()
            (cov_copy(dx, False) if dx else cov_local()).start()

    loads[1].wait()
    lt[0:256, :] = b5[...].reshape(1024, 256).T
    loads[2].wait()

    def turn(i, _):
        block = a5[pl.ds(i, 1)].reshape(128, 1024)
        at5[:, :, :, :, pl.ds(pl.multiple_of(i * 128, 128), 128)] = block.T.reshape(8, 4, 2, 16, 128)
        return 0

    lax.fori_loop(0, 8, turn, 0)
    lt[256:320, :] = at5[z, :, c].reshape(64, 1024)

    for cp in swap:
        cp.wait_recv()
    wsum = wt[...] + wr[...]
    for q in range(4):
        e = (mine[q, c] + theirs[q]) / wsum[q : q + 1, 0:1]
        high = e.astype(BF16)
        eb[q, :, 0:1024] = high
        mine[q, c] = e - high.astype(F32)
    for q in range(4):
        eb[q, :, 1024:1152] = mine[q, c, :, pl.ds(zlane, 128)].astype(BF16)

    spread_e = [
        remote(eb.at[xs(dx)], e5.at[z, x, c], sb_s.at[dx], sb_r.at[dx], dev(c, z, xs(dx)))
        for dx in (2, 1, 3)
    ]
    for cp in spread_e:
        cp.start()
    e5[z, x, c] = eb[x]
    for dx in (2, 1, 3):
        remote(eb.at[xs(dx)], e5.at[z, xs(-dx), c], sb_s.at[dx], sb_r.at[dx], dev(c, z, xs(dx))).wait_recv()

    def ring_copy(buf, ssem, rsem, d, s, h):
        sign = 1 - 2 * d
        part = buf.at[zs(-sign * (s - 1)), pl.ds(2 * h, 2), c]
        return remote(part, part, ssem.at[d, s - 1, h], rsem.at[d, s - 1, h], dev(c, zs(sign), x))

    def ring_got(buf, ssem, rsem, d, s, h):
        sign = 1 - 2 * d
        part = buf.at[zs(-sign * s), pl.ds(2 * h, 2), c]
        return remote(part, part, ssem.at[d, s - 1, h], rsem.at[d, s - 1, h], dev(c, zs(sign), x))

    def hand(buf, ssem, rsem, d, s, h, core):
        sign = 1 - 2 * d
        part = buf.at[zs(-sign * s), pl.ds(2 * h, 2), core]
        return remote(part, part, ssem.at[d, s, h], rsem.at[d, s, h], pair)

    def ring_start(buf, ssem, rsem, fs, fr):
        for h in range(2):
            for d in ((0, 1) if h == 0 else (1, 0)):
                ring_copy(buf, ssem, rsem, d, 1, h).start()
        for h in range(2):
            hand(buf, fs, fr, 0, 0, h, c).start()

    def ring_step(buf, ssem, rsem, fs, fr, s):
        for h in range(2):
            for d in ((0, 1) if h == 0 else (1, 0)):
                if s <= HOPS[d][h]:
                    ring_got(buf, ssem, rsem, d, s, h).wait_recv()
                    if s < HOPS[d][h]:
                        ring_copy(buf, ssem, rsem, d, s + 1, h).start()
                    hand(buf, fs, fr, d, s, h, c).start()

    def hand_wait(buf, fs, fr, s):
        for h in range(2):
            if s == 0:
                hand(buf, fs, fr, 0, 0, h, oc).wait_recv()
            else:
                for d in range(2):
                    if s <= HOPS[d][h]:
                        hand(buf, fs, fr, d, s, h, oc).wait_recv()

    def drain(buf, ssem, rsem, fs, fr):
        for h in range(2):
            hand(buf, fs, fr, 0, 0, h, c).wait_send()
            for d in range(2):
                for s in range(1, HOPS[d][h] + 1):
                    ring_copy(buf, ssem, rsem, d, s, h).wait_send()
                    hand(buf, fs, fr, d, s, h, c).wait_send()

    e_ring = (e5, er_s, er_r, ef_s, ef_r)
    p_ring = (p5, pr_s, pr_r, pf_s, pf_r)

    def gather_add(zc, begin):
        k = pl.ds(pl.multiple_of(zc * 128, 128), 128)
        left = lt[:, k]

        def part(i, _):
            cols = pl.ds(pl.multiple_of(i * 256, 256), 256)
            v = mm(left, e5[zc, :, :, :, cols].reshape(128, 256))
            acc[:, cols] = v if begin else acc[:, cols] + v
            return 0

        lax.fori_loop(0, 4, part, 0)
        acc[:, k] += mm(left, e5[zc, :, :, :, 1024:1152].reshape(128, 128))

    ring_start(*e_ring)
    hand_wait(e5, ef_s, ef_r, 0)
    gather_add(z, True)
    for s in range(1, 5):
        ring_step(*e_ring, s)
        if s == 4:
            for dx in (2, 1, 3):
                remote(pcov.at[0, 0:16], p5.at[z, xs(-dx), c], pa_s.at[dx, 0], pa_r.at[dx], pair).wait_recv()

            @pl.when(own == c)
            def _():
                cov_local().wait()

            @pl.when(own != c)
            def _():
                remote(pcov.at[0, 0:16], p5.at[z, x, c], pa_s.at[0, 0], pa_r.at[0], pair).wait_recv()

            ring_start(*p_ring)
        hand_wait(e5, ef_s, ef_r, s)
        if s < 4:
            gather_add(zs(-s), False)
            gather_add(zs(s), False)
        else:
            gather_add(zs(4), False)

    hi, lo = split(acc[...])
    bh[...] = hi
    bl[...] = lo
    bfull = b5[...].reshape(1024, 256)
    small = mm(bh[...], bfull) + mm(bl[...], bfull)
    weights = jnp.where(own == c, iw[pl.ds(jq, 1), :], iwr[pl.ds(jq, 1), :])
    r256 = lax.broadcasted_iota(jnp.int32, (256, 256), 0)
    c256 = lax.broadcasted_iota(jnp.int32, (256, 256), 1)
    curv = small[0:256] + jnp.where(r256 == c256, weights, 0.0)
    cpl_own = split(small[256:320])

    def times_a(i, _):
        cols = pl.ds(pl.multiple_of(i * 256, 256), 256)
        right = a5[:, :, :, :, cols].reshape(1024, 256)
        cpl[:, cols] = mm(bh[...], right) + mm(bl[...], right)
        return 0

    lax.fori_loop(0, 4, times_a, 0)

    ring_step(*p_ring, 1)
    s11, s12, s22 = curv[:128, :128], curv[:128, 128:], curv[128:, 128:]
    inv = sweep(s11, 8)
    ring_step(*p_ring, 2)
    inv = sweep(inv, 8)
    ring_step(*p_ring, 3)
    inv_s, s12_s = split(inv), split(s12)
    w_s = split(mm3(inv_s, s12_s))
    inv2 = sweep(s22 - mm3(s12_s, w_s, ((0,), (0,))), 8)
    ring_step(*p_ring, 4)
    inv2_s = split(sweep(inv2, 8))

    def back(i, _):
        cols = pl.ds(pl.multiple_of(i * 256, 256), 256)
        top = split(cpl[0:128, cols])
        low = cpl[128:256, cols] - mm3(w_s, top, ((0,), (0,)))
        g2 = mm3(inv2_s, split(low))
        g1 = mm3(inv_s, top) - mm3(w_s, split(g2))
        gv[0:128, cols] = g1
        gv[128:256, cols] = g2
        for half, g in ((0, g1), (128, g2)):
            high, rest = split(g)
            gh[half : half + 128, cols] = high
            gl[half : half + 128, cols] = rest
        return 0

    lax.fori_loop(0, 4, back, 0)

    def gain_copy(dx):
        xx = xs(dx)
        rows = pl.ds(pl.multiple_of(32 * z + 8 * xx, 8), 8)
        return remote(gv.at[rows], pgr.at[jq], gs_s.at[dx], gs_r.at[dx], dev(c, z, xx))

    @pl.when(own == c)
    def _():
        for dx in (2, 1, 3):
            gain_copy(dx).start()
        pgr[jq] = gv[pl.ds(pl.multiple_of(32 * z + 8 * x, 8), 8), :]

    def cost(i, _):
        cols = pl.ds(pl.multiple_of(i * 256, 256), 256)
        v = cpl[256:320, cols] - mm3(cpl_own, (gh[:, cols], gl[:, cols]))
        pcv[:, :, cols] = v.reshape(4, 16, 256)
        return 0

    lax.fori_loop(0, 4, cost, 0)

    def cost_copy(dx):
        return remote(pcv.at[xs(dx)], pcr.at[jq, c], cs_s.at[dx], cs_r.at[dx, c], dev(own, z, xs(dx)))

    for dx in (2, 1, 3):
        cost_copy(dx).start()

    @pl.when(own == c)
    def _():
        pcr[jq, c] = pcv[x]

    @pl.when(own != c)
    def _():
        cost_copy(0).start()

    a_rows = a5[z, :, c].reshape(64, 1024).astype(F32)
    b_rows = b5[z, :, c].reshape(64, 256)
    closed = (a_rows - (mm(b_rows, gh[...]) + mm(b_rows, gl[...]))).astype(BF16)
    for s in range(5):
        hand_wait(p5, pf_s, pf_r, s)
    moment_s = split(mm(closed, p5[...].reshape(1024, 1024)))
    nt = ((1,), (1,))
    inner_s = split(mm3(moment_s, (gh[...], gl[...]), nt))

    def out_cols(i, _):
        cols = pl.ds(pl.multiple_of(i * 256, 256), 256)
        v = mm2(moment_s, at5[:, :, :, :, cols].reshape(1024, 256)) - mm2(inner_s, lt[0:256, cols])
        spv[:, :, cols] = v.reshape(4, 16, 256)
        return 0

    lax.fori_loop(0, 4, out_cols, 0)

    def spread_copy(dx):
        return remote(spv.at[xs(dx)], spr.at[x, c], ss_s.at[dx], ss_r.at[dx], dev(c, z, xs(dx)))

    def spread_got(dx):
        return remote(spv.at[xs(dx)], spr.at[xs(-dx), c], ss_s.at[dx], ss_r.at[dx], dev(c, z, xs(dx)))

    def spread_hand(dx, core):
        return remote(spr.at[xs(-dx), core], spr.at[xs(-dx), core], sf_s.at[dx], sf_r.at[dx], pair)

    for dx in (2, 1, 3):
        spread_copy(dx).start()
    spr[x, c] = spv[x]
    spread_hand(0, c).start()

    for dx in (1, 2, 3):
        @pl.when(xs(-dx) // 2 == c)
        def _(dx=dx):
            remote(gv.at[0:8], pgr.at[lax.rem(xs(-dx), 2)], gs_s.at[dx], gs_r.at[dx], pair).wait_recv()
            for core in range(2):
                remote(pcv.at[0], pcr.at[lax.rem(xs(-dx), 2), core], cs_s.at[dx], cs_r.at[dx, core], pair).wait_recv()

    @pl.when(own == c)
    def _():
        remote(pcv.at[0], pcr.at[jq, oc], cs_s.at[0], cs_r.at[0, oc], pair).wait_recv()

    out_pg = pltpu.make_async_copy(pgr, pg_out, out_sem.at[8])
    out_pg.start()
    diag = lax.broadcasted_iota(jnp.int32, (32, 128), 1) == (
        32 * x + lax.broadcasted_iota(jnp.int32, (32, 128), 0)
    )
    pick = lax.broadcasted_iota(jnp.int32, (32, 32), 1) == lax.broadcasted_iota(jnp.int32, (32, 32), 0)

    def on_diag(row):
        column = jnp.sum(jnp.where(pick, row, 0.0), axis=1, keepdims=True)
        return jnp.where(diag, column, 0.0)

    for j in range(2):
        pcr[j, :, :, pl.ds(zlane, 128)] += on_diag(sw[j : j + 1, :]).reshape(2, 16, 128)
    out_pc = pltpu.make_async_copy(pcr, pc_out, out_sem.at[9])
    out_pc.start()

    for dx in (1, 3, 2):
        spread_got(dx).wait_recv()
        spread_hand(dx, c).start()
    for dx in range(4):
        spread_hand(dx, oc).wait_recv()

    pos = [[po[k] == first + q for q in range(4)] for k in range(8)]
    outs = []
    for k in range(8):
        def fill(i, _, k=k):
            cols = pl.ds(pl.multiple_of(i * 256, 256), 256)
            v = spr[0, :, :, cols]
            for q in range(1, 4):
                v = jnp.where(pos[k][q], spr[q, :, :, cols], v)
            chv[k, :, :, cols] = v
            return 0

        lax.fori_loop(0, 4, fill, 0)
        chv[k, :, :, pl.ds(zlane, 128)] += on_diag(nz[k : k + 1, :]).reshape(2, 16, 128)
        cp = pltpu.make_async_copy(chv.at[k], ch_out.at[k], out_sem.at[k])
        cp.start()
        outs.append(cp)

    for cp in swap + spread_e:
        cp.wait_send()
    for dx in range(4):
        @pl.when(xs(dx) // 2 == c)
        def _(dx=dx):
            cov_copy(dx, True).wait_send()
            if dx:
                cov_copy(dx, False).wait_send()
    drain(*e_ring)
    drain(*p_ring)

    @pl.when(own == c)
    def _():
        for dx in (2, 1, 3):
            gain_copy(dx).wait_send()

    @pl.when(own != c)
    def _():
        cost_copy(0).wait_send()

    for dx in (2, 1, 3):
        cost_copy(dx).wait_send()
        spread_copy(dx).wait_send()
    for dx in range(4):
        spread_hand(dx, c).wait_send()
    out_pg.wait()
    out_pc.wait()
    for cp in outs:
        cp.wait()


def on_device(cc, cw, po, a, b, sw, iw, pcov, nz):
    any_, vmem, smem = (pl.BlockSpec(memory_space=m) for m in (pl.ANY, pltpu.VMEM, pltpu.SMEM))
    v, dma = pltpu.VMEM, pltpu.SemaphoreType.DMA
    scratch = [
        v((8, 32, 1024), F32),
        v((8, 4, 2, 16, 1024), BF16),
        v((8, 4, 2, 16, 256), BF16),
        v((8, 4, 2, 16, 1024), BF16),
        v((320, 1024), BF16),
        v((8, 4, 2, 16, 1152), BF16),
        v((8, 4, 2, 16, 1024), BF16),
        v((320, 1024), F32),
        v((4, 2, 16, 1024), F32),
        v((4, 16, 1024), F32),
        v((8, 128), F32),
        v((8, 128), F32),
        v((2, 256), F32),
        v((4, 16, 1152), BF16),
        v((320, 1024), BF16),
        v((320, 1024), BF16),
        v((320, 1024), F32),
        v((256, 1024), F32),
        v((256, 1024), BF16),
        v((256, 1024), BF16),
        v((4, 16, 1024), F32),
        v((2, 2, 16, 1024), F32),
        v((2, 8, 1024), F32),
        v((4, 16, 1024), F32),
        v((4, 2, 16, 1024), F32),
        v((8, 2, 16, 1024), F32),
        dma((3,)), dma((1,)), dma((10,)),
        dma((3,)), dma((3,)),
        dma((4,)), dma((4,)),
        dma((4, 2)), dma((4,)),
        dma((2, 4, 2)), dma((2, 4, 2)), dma((2, 5, 2)), dma((2, 5, 2)),
        dma((2, 4, 2)), dma((2, 4, 2)), dma((2, 5, 2)), dma((2, 5, 2)),
        dma((4,)), dma((4,)),
        dma((4,)), dma((4, 2)),
        dma((4,)), dma((4,)), dma((4,)), dma((4,)),
    ]
    pc, pg, ch = pl.pallas_call(
        kernel,
        out_shape=(
            jax.ShapeDtypeStruct((2, 2, 16, 1024), F32),
            jax.ShapeDtypeStruct((2, 8, 1024), F32),
            jax.ShapeDtypeStruct((8, 2, 16, 1024), F32),
        ),
        in_specs=[any_, smem, smem, any_, any_, vmem, vmem, vmem, vmem],
        out_specs=(any_, any_, any_),
        scratch_shapes=scratch,
        compiler_params=pltpu.CompilerParams(collective_id=0, has_side_effects=True),
    )(
        cc, cw, po, a.reshape(8, 4, 2, 16, 1024), b.reshape(8, 4, 2, 16, 256), sw, iw, pcov, nz
    )
    return pc.reshape(2, 32, 1024), pg, ch.reshape(8, 32, 1024)


def solution(mesh):
    rows = P("node", "tile", None)
    placed = (rows, P("node"), P("node"), P(), P(), P("node", "tile"), P("node", None), rows, P("node", "tile"))
    return jax.shard_map(
        on_device, mesh=mesh, in_specs=placed, out_specs=(rows, rows, rows), check_vma=False
    )
```

profile of v0, /device:TPU:1, one launch (start us, length us, event | category | flops | bytes accessed | tf_op | source)
XLA Modules:
  0.0 77.8 jit_solution(15486393905603262344)
XLA Ops:
  0.6 71.7 %shard_map.112 = (f32[2,2,16,1024]{3,2,1,0:T(8,128)}, f32[2,8,1024]{2,1,0:T(8,128)}, f32[8,2,16,1024]{3,2,1,0:T(8,128)}) custom-call(f32[8,32,1024]{2,1,0:T(8,128)} %cc.1, s32[8]{0:T(128)} %cw.1, s32[8]{0:T(128)} %po.1, bf16[8,4,2,16,1024]{4,3,2,1,0:T(8,128)(2,1)} %bitcast.4, bf16[8,4,2,16,256]{4,3,2,1,0:T(8,128)(2,1)} %bitcast.6, f32[2,32]{1,0:T(2,128)} %sw.1, ...), custom_call_target="tpu_custom_call" | custom-call | tf_op jit(solution)/shard_map/pallas_call | solution.py:559
  72.4 1.7 %copy.15 = f32[2,32,1024]{2,1,0:T(8,128)} copy(f32[2,32,1024]{2,1,0:T(8,128)} %bitcast.7) | data formatting | bytes 524288
  74.1 1.5 %copy.16 = f32[2,8,1024]{2,1,0:T(8,128)} copy(f32[2,8,1024]{2,1,0:T(8,128)} %get-tuple-element.13) | data formatting | bytes 131072
  75.5 2.3 %copy.17 = f32[8,32,1024]{2,1,0:T(8,128)} copy(f32[8,32,1024]{2,1,0:T(8,128)} %bitcast.5) | data formatting | bytes 2097152
where the time goes:
time: 78.1 us; the launch traced here: 77.8 us
  Pallas kernels  71.7 us (92%)
  local copies, waits for them, and re-layouts  5.45 us (7%)
    pallas_call x1, Pallas kernels, on_device(): pl.pallas_call(kernel, out_shape=(jax.ShapeDtypeStruct((2, 2, 16, 1024),...  71.7 us
    unnamed x3, local copies, waits for them, and re-layouts  5.45 us

commit v1 on v0

v1 whole, which is shorter than its diff:
```python
import functools

import jax
import jax.numpy as jnp
from jax import lax
from jax.experimental import pallas as pl
from jax.experimental.pallas import tpu as pltpu
from jax.sharding import PartitionSpec as P

F32, BF16 = jnp.float32, jnp.bfloat16
MESH = pl.DeviceIdType.MESH


def split(v):
    high = v.astype(BF16)
    return high, (v - high.astype(F32)).astype(BF16)


def mm(a, b, dims=((1,), (0,))):
    return lax.dot_general(a, b, (dims, ((), ())), preferred_element_type=F32)


def mm2(a, b, dims=((1,), (0,))):
    return mm(a[0], b, dims) + mm(a[1], b, dims)


def mm3(a, b, dims=((1,), (0,))):
    return mm(a[0], b[0], dims) + (mm(a[0], b[1], dims) + mm(a[1], b[0], dims))


def total(terms):
    while len(terms) > 1:
        terms = [
            terms[i] + terms[i + 1] if i + 1 < len(terms) else terms[i]
            for i in range(0, len(terms), 2)
        ]
    return terms[0]


def small_inverse(d):
    b = len(d)
    if b == 2:
        r = 1.0 / (d[0][0] * d[1][1] - d[0][1] * d[0][1])
        off = -d[0][1] * r
        return [[d[1][1] * r, off], [off, d[0][0] * r]]
    h = b // 2
    span = range(h)
    x = small_inverse([[d[i][j] for j in span] for i in span])
    y = [[d[i][h + j] for j in span] for i in span]
    w = [[total([x[i][k] * y[k][j] for k in span]) for j in span] for i in span]
    s = [[None] * h for _ in span]
    for i in span:
        for j in range(i, h):
            s[i][j] = s[j][i] = d[h + i][h + j] - total([y[k][i] * w[k][j] for k in span])
    q = small_inverse(s)
    wq = [[total([w[i][k] * q[k][j] for k in span]) for j in span] for i in span]
    out = [[None] * b for _ in range(b)]
    for i in span:
        for j in range(i, h):
            out[i][j] = out[j][i] = x[i][j] + total([wq[i][k] * w[j][k] for k in span])
        for j in span:
            out[i][h + j] = out[h + j][i] = -wq[i][j]
            out[h + i][h + j] = q[i][j]
    return out


def sweep(a, trips, beside=None, b=4, unroll=8):
    n = a.shape[0]
    lane = lax.broadcasted_iota(jnp.int32, (1, n), 1)
    lanes = lax.broadcasted_iota(jnp.int32, (n, n), 1)
    sub = lax.broadcasted_iota(jnp.int32, (n, 1), 0)

    def body(trip, a):
        if beside is not None:
            beside(trip)
        for low in range(0, unroll, b):
            ks = range(low, low + b)
            d = [[jnp.broadcast_to(a[i : i + 1, j : j + 1], (1, n)) for j in ks] for i in ks]
            inv = small_inverse(d)
            rows = [a[j : j + 1, :] for j in ks]
            in_rows = (sub >= low) & (sub < low + b)
            cols = [jnp.where(sub == k, -1.0, jnp.where(in_rows, 0.0, a[:, k : k + 1])) for k in ks]
            new = []
            for i in range(b):
                t = total([inv[i][j] * rows[j] for j in range(b)])
                for j in range(b):
                    t = jnp.where(lane == low + j, inv[i][j], t)
                new.append(t)
            a = jnp.where(((lanes >= low) & (lanes < low + b)) | in_rows, 0.0, a)
            for i in range(b):
                a = a - cols[i] * new[i]
        a = jnp.concatenate([a[unroll:], a[:unroll]], axis=0)
        return pltpu.roll(a, n - unroll, 1)

    return lax.fori_loop(0, trips, body, a)


ORDER = (0, 1, 3, 2)
HOPS = ((4, 3, 3, 4), (3, 4, 4, 3))
BLOCKS = 5


def place():
    n, t = lax.axis_index("node"), lax.axis_index("tile")
    return lax.rem(n, 2), n // 2, t // 4, lax.rem(t, 4)


def kernel(
    cw, po, cc, a_in, b_in, iw_in, pcov_in,
    pcr_out, pgr_out, spr_out,
    ccv, a5, b5, at5, lt, e5, p5, acc, mine, theirs, wt, wr, iw, iwr, pcov, pk, eb,
    bh, bl, cpl, gv, gh, gl, cl2, mom, pcv, pcr, pgr, spv, spr,
    load_sem, loc_sem, out_sem, sa_s, sa_r, sb_s, sb_r, pa_s, pa_r,
    er_s, er_r, ef_s, ef_r, pr_s, pr_r, pf_s, pf_r,
    gs_s, gs_r, cs_s, cs_r, ss_s, ss_r, sf_s, sf_r,
):
    c, y, z, x = place()
    oc = 1 - c
    own, jq = x // 2, lax.rem(x, 2)

    def dev(core, zz, xx):
        return (2 * y + core, 4 * zz + xx)

    def xs(dx):
        return lax.rem(x + dx + 4, 4)

    def zs(dz):
        return lax.rem(z + dz + 8, 8)

    def remote(src, dst, ssem, rsem, where):
        return pltpu.make_async_remote_copy(
            src_ref=src, dst_ref=dst, send_sem=ssem, recv_sem=rsem,
            device_id=where, device_id_type=MESH,
        )

    def lanes(block):
        return pl.ds(pl.multiple_of(lax.rem(block, 8) * 128, 128), 128)

    barrier = pltpu.get_barrier_semaphore()
    for dx in range(4):
        for core in ((oc,) if dx == 0 else (c, oc)):
            pl.semaphore_signal(barrier, inc=1, device_id=dev(core, z, xs(dx)), device_id_type=MESH)
    for dz in (1, -1):
        pl.semaphore_signal(barrier, inc=1, device_id=dev(c, zs(dz), x), device_id_type=MESH)

    loads = [
        pltpu.make_async_copy(cc, ccv, load_sem.at[0]),
        pltpu.make_async_copy(b_in, b5, load_sem.at[1]),
        pltpu.make_async_copy(a_in, a5, load_sem.at[2]),
        pltpu.make_async_copy(iw_in, iw, load_sem.at[3]),
        pltpu.make_async_copy(pcov_in, pcov, load_sem.at[4]),
    ]
    for cp in loads:
        cp.start()

    first = 4 * y
    coef = [
        [jnp.where(po[k] == first + q, cw[k].astype(F32), 0.0) for q in range(4)]
        for k in range(8)
    ]
    sub8 = lax.broadcasted_iota(jnp.int32, (8, 128), 0)
    tile = jnp.zeros((8, 128), F32)
    for q in range(4):
        s = total([coef[k][q] for k in range(8)])
        tile = jnp.where(sub8 == q, s, tile)
    wt[...] = tile

    loads[0].wait()

    def weigh(i, _):
        cols = pl.ds(pl.multiple_of(i * 256, 256), 256)
        for h in range(2):
            sums = [None] * 4
            for k in range(8):
                v = ccv[k, 16 * h : 16 * h + 16, cols]
                for q in range(4):
                    term = coef[k][q] * v
                    sums[q] = term if k == 0 else sums[q] + term
            for q in range(4):
                mine[q, h, :, cols] = sums[q]
        return 0

    lax.fori_loop(0, 4, weigh, 0)

    loads[3].wait()
    pl.semaphore_wait(barrier, 9)

    pair = dev(oc, z, x)
    swap = [
        remote(mine.at[:, oc], theirs, sa_s.at[0], sa_r.at[0], pair),
        remote(wt, wr, sa_s.at[1], sa_r.at[1], pair),
        remote(iw, iwr, sa_s.at[2], sa_r.at[2], pair),
    ]
    for cp in swap:
        cp.start()

    loads[1].wait()
    lt[0:256, 0:1024] = b5[...].reshape(1024, 256).T
    loads[2].wait()

    def turn(i, _):
        block = a5[pl.ds(i, 1)].reshape(128, 1024)
        at5[:, :, :, :, pl.ds(pl.multiple_of(i * 128, 128), 128)] = block.T.reshape(8, 4, 2, 16, 128)
        return 0

    lax.fori_loop(0, 8, turn, 0)
    lt[256:320, 0:1024] = at5[z, :, c].reshape(64, 1024)
    lt[:, 1024:1536] = lt[:, 0:512]
    loads[4].wait()
    for p in range(BLOCKS):
        pk[:, :, 128 * p : 128 * p + 128] = pcov[:, :, lanes(z + p)]

    for cp in swap:
        cp.wait_recv()
    wsum = wt[...] + wr[...]
    for q in range(4):
        w = wsum[q : q + 1, 0:1]
        for p in range(BLOCKS):
            e = (mine[q, c, :, lanes(z + p)] + theirs[q, :, lanes(z + p)]) / w
            high = e.astype(BF16)
            eb[q, :, 128 * p : 128 * p + 128] = high
            if p == 0:
                eb[q, :, 128 * BLOCKS :] = (e - high.astype(F32)).astype(BF16)

    spread_e = [
        remote(eb.at[xs(dx)], e5.at[z, x, c], sb_s.at[dx], sb_r.at[dx], dev(c, z, xs(dx)))
        for dx in (2, 1, 3)
    ]
    for cp in spread_e:
        cp.start()
    e5[z, x, c] = eb[x]

    def cov_copy(dx, other):
        q = xs(dx)
        core = oc if other else c
        return remote(
            pk.at[lax.rem(q, 2), pl.ds(pl.multiple_of(16 * core, 16), 16)],
            p5.at[z, x, core], pa_s.at[dx, int(other)], pa_r.at[dx], dev(core, z, q),
        )

    def cov_local():
        return pltpu.make_async_copy(
            pk.at[jq, pl.ds(pl.multiple_of(16 * c, 16), 16)], p5.at[z, x, c], loc_sem.at[0]
        )

    def cov_start():
        for dx in (2, 1, 3, 0):
            @pl.when(xs(dx) // 2 == c)
            def _(dx=dx):
                cov_copy(dx, True).start()
                (cov_copy(dx, False) if dx else cov_local()).start()

    def cov_wait():
        for dx in (2, 1, 3):
            remote(pk.at[0, 0:16], p5.at[z, xs(-dx), c], pa_s.at[dx, 0], pa_r.at[dx], pair).wait_recv()

        @pl.when(own == c)
        def _():
            cov_local().wait()

        @pl.when(own != c)
        def _():
            remote(pk.at[0, 0:16], p5.at[z, x, c], pa_s.at[0, 0], pa_r.at[0], pair).wait_recv()

    def ring(buf, ssem, rsem, d, s, h, got):
        sign = 1 - 2 * d
        part = buf.at[zs(-sign * (s if got else s - 1)), xs(-h), c]
        return remote(part, part, ssem.at[d, s - 1, h], rsem.at[d, s - 1, h], dev(c, zs(sign), x))

    def hand(buf, fs, fr, d, s, h, core):
        sign = 1 - 2 * d
        part = buf.at[zs(-sign * s), xs(-h), core]
        return remote(part, part, fs.at[d, s, h], fr.at[d, s, h], pair)

    def ring_start(buf, ssem, rsem, fs, fr, h):
        for d in (0, 1):
            ring(buf, ssem, rsem, d, 1, h, False).start()
        hand(buf, fs, fr, 0, 0, h, c).start()

    def ring_step(buf, ssem, rsem, fs, fr, s, pieces=ORDER):
        for h in pieces:
            for d in (0, 1):
                if s <= HOPS[d][h]:
                    ring(buf, ssem, rsem, d, s, h, True).wait_recv()
                    if s < HOPS[d][h]:
                        ring(buf, ssem, rsem, d, s + 1, h, False).start()
                    hand(buf, fs, fr, d, s, h, c).start()

    def hand_wait(buf, fs, fr, s):
        for h in ORDER:
            for d in (0,) if s == 0 else (0, 1):
                if s <= HOPS[d][h]:
                    hand(buf, fs, fr, d, s, h, oc).wait_recv()

    def drain(buf, ssem, rsem, fs, fr):
        for h in ORDER:
            hand(buf, fs, fr, 0, 0, h, c).wait_send()
            for d in range(2):
                for s in range(1, HOPS[d][h] + 1):
                    ring(buf, ssem, rsem, d, s, h, False).wait_send()
                    hand(buf, fs, fr, d, s, h, c).wait_send()

    e_ring = (e5, er_s, er_r, ef_s, ef_r)
    p_ring = (p5, pr_s, pr_r, pf_s, pf_r)

    def chunk_add(buf, zc, left2, out):
        left = left2[:, lanes(zc)]
        chunk = buf[zc].reshape(128, buf.shape[-1])
        for p in range(BLOCKS):
            v = mm(left, chunk[:, 128 * p : 128 * p + 128])
            if p == 0 and buf.shape[-1] > 128 * BLOCKS:
                v = v + mm(left, chunk[:, 128 * BLOCKS :])
            out[:, lanes(zc + p)] += v
        turned = left2[:, pl.ds(pl.multiple_of(128 * zc + 128, 128), 384)]
        out[:, lanes(zc)] += mm(turned, chunk[:, 128:512], ((1,), (1,)))

    ring_start(*e_ring, 0)
    acc[...] = jnp.zeros_like(acc)
    for dx in ORDER[1:]:
        remote(eb.at[xs(dx)], e5.at[z, xs(-dx), c], sb_s.at[dx], sb_r.at[dx], dev(c, z, xs(dx))).wait_recv()
        ring_start(*e_ring, dx)
    cov_start()
    for s in range(1, 5):
        ring_step(*e_ring, s, ORDER[:2])
        hand_wait(e5, ef_s, ef_r, s - 1)
        chunk_add(e5, zs(1 - s), lt, acc)
        ring_step(*e_ring, s, ORDER[2:])
        if s > 1:
            chunk_add(e5, zs(s - 1), lt, acc)
    cov_wait()
    for h in ORDER:
        ring_start(*p_ring, h)
    hand_wait(e5, ef_s, ef_r, 4)
    chunk_add(e5, zs(4), lt, acc)

    hi, lo = split(acc[...])
    bh[...] = hi
    bl[...] = lo
    bfull = b5[...].reshape(1024, 256)
    small = mm(bh[...], bfull) + mm(bl[...], bfull)
    weights = jnp.where(own == c, iw[pl.ds(jq, 1), :], iwr[pl.ds(jq, 1), :])
    r256 = lax.broadcasted_iota(jnp.int32, (256, 256), 0)
    c256 = lax.broadcasted_iota(jnp.int32, (256, 256), 1)
    curv = small[0:256] + jnp.where(r256 == c256, weights, 0.0)
    cpl_own = split(small[256:320])

    def times_a(trip):
        rows = pl.ds(pl.multiple_of(lax.rem(trip, 2) * 160, 32), 160)
        cols = pl.ds(pl.multiple_of((trip // 2) * 256, 256), 256)
        right = a5[:, :, :, :, cols].reshape(1024, 256)
        cpl[rows, cols] = mm(bh[rows, :], right) + mm(bl[rows, :], right)

    s11, s12, s22 = curv[:128, :128], curv[:128, 128:], curv[128:, 128:]
    inv = sweep(s11, 8, times_a)
    ring_step(*p_ring, 1)
    inv = sweep(inv, 8)
    ring_step(*p_ring, 2)
    inv_s, s12_s = split(inv), split(s12)
    w = mm3(inv_s, s12_s)
    w_s = split(w)
    inv2 = sweep(s22 - mm3(s12_s, w_s, ((0,), (0,))), 8)
    ring_step(*p_ring, 3)
    inv2 = sweep(inv2, 8)
    ring_step(*p_ring, 4)
    wq = mm3(w_s, split(inv2))
    inv1 = inv + mm3(split(wq), w_s, ((1,), (1,)))
    full_s = split(
        jnp.concatenate(
            [jnp.concatenate([inv1, -wq], axis=1), jnp.concatenate([-wq.T, inv2], axis=1)], axis=0
        )
    )

    def back(i, _):
        cols = pl.ds(pl.multiple_of(i * 256, 256), 256)
        g = mm3(full_s, split(cpl[0:256, cols]))
        gv[:, cols] = g
        gh[:, cols], gl[:, cols] = split(g)
        return 0

    lax.fori_loop(0, 4, back, 0)

    def gain_copy(dx):
        xx = xs(dx)
        rows = pl.ds(pl.multiple_of(32 * z + 8 * xx, 8), 8)
        return remote(gv.at[rows], pgr.at[jq], gs_s.at[dx], gs_r.at[dx], dev(c, z, xx))

    @pl.when(own == c)
    def _():
        for dx in (2, 1, 3):
            gain_copy(dx).start()
        pgr[jq] = gv[pl.ds(pl.multiple_of(32 * z + 8 * x, 8), 8), :]

    def cost(i, _):
        cols = pl.ds(pl.multiple_of(i * 256, 256), 256)
        v = cpl[256:320, cols] - mm3(cpl_own, (gh[:, cols], gl[:, cols]))
        pcv[:, :, cols] = v.reshape(4, 16, 256)
        return 0

    lax.fori_loop(0, 4, cost, 0)

    def cost_copy(dx):
        return remote(pcv.at[xs(dx)], pcr.at[jq, c], cs_s.at[dx], cs_r.at[dx, c], dev(own, z, xs(dx)))

    for dx in (2, 1, 3):
        cost_copy(dx).start()

    @pl.when(own == c)
    def _():
        pcr[jq, c] = pcv[x]

    @pl.when(own != c)
    def _():
        cost_copy(0).start()

    a_rows = a5[z, :, c].reshape(64, 1024).astype(F32)
    b_rows = b5[z, :, c].reshape(64, 256)
    closed = (a_rows - (mm(b_rows, gh[...]) + mm(b_rows, gl[...]))).astype(BF16)
    cl2[:, 0:1024] = closed
    cl2[:, 1024:1536] = closed[:, 0:512]
    mom[...] = jnp.zeros_like(mom)
    for s in range(5):
        hand_wait(p5, pf_s, pf_r, s)

    def moment(i, _):
        chunk_add(p5, i, cl2, mom)
        return 0

    lax.fori_loop(0, 8, moment, 0)
    moment_s = split(mom[...])
    nt = ((1,), (1,))
    inner_s = split(mm3(moment_s, (gh[...], gl[...]), nt))

    def out_cols(i, _):
        cols = pl.ds(pl.multiple_of(i * 256, 256), 256)
        v = mm2(moment_s, at5[:, :, :, :, cols].reshape(1024, 256)) - mm2(inner_s, lt[0:256, cols])
        spv[:, :, cols] = v.reshape(4, 16, 256)
        return 0

    lax.fori_loop(0, 4, out_cols, 0)

    def spread_copy(dx):
        return remote(spv.at[xs(dx)], spr.at[x, c], ss_s.at[dx], ss_r.at[dx], dev(c, z, xs(dx)))

    def spread_got(dx):
        return remote(spv.at[xs(dx)], spr.at[xs(-dx), c], ss_s.at[dx], ss_r.at[dx], dev(c, z, xs(dx)))

    def spread_hand(dx, core):
        return remote(spr.at[xs(-dx), core], spr.at[xs(-dx), core], sf_s.at[dx], sf_r.at[dx], pair)

    for dx in (2, 1, 3):
        spread_copy(dx).start()
    spr[x, c] = spv[x]
    spread_hand(0, c).start()

    for dx in (1, 2, 3):
        @pl.when(xs(-dx) // 2 == c)
        def _(dx=dx):
            remote(gv.at[0:8], pgr.at[lax.rem(xs(-dx), 2)], gs_s.at[dx], gs_r.at[dx], pair).wait_recv()
            for core in range(2):
                remote(pcv.at[0], pcr.at[lax.rem(xs(-dx), 2), core], cs_s.at[dx], cs_r.at[dx, core], pair).wait_recv()

    @pl.when(own == c)
    def _():
        remote(pcv.at[0], pcr.at[jq, oc], cs_s.at[0], cs_r.at[0, oc], pair).wait_recv()

    out_pg = pltpu.make_async_copy(pgr, pgr_out, out_sem.at[0])
    out_pg.start()
    out_pc = pltpu.make_async_copy(pcr, pcr_out, out_sem.at[1])
    out_pc.start()

    for dx in (1, 3, 2):
        spread_got(dx).wait_recv()
        spread_hand(dx, c).start()
    for dx in range(4):
        spread_hand(dx, oc).wait_recv()

    out_sp = pltpu.make_async_copy(spr, spr_out, out_sem.at[2])
    out_sp.start()

    for cp in swap + spread_e:
        cp.wait_send()
    for dx in range(4):
        @pl.when(xs(dx) // 2 == c)
        def _(dx=dx):
            cov_copy(dx, True).wait_send()
            if dx:
                cov_copy(dx, False).wait_send()
    drain(*e_ring)
    drain(*p_ring)

    @pl.when(own == c)
    def _():
        for dx in (2, 1, 3):
            gain_copy(dx).wait_send()

    @pl.when(own != c)
    def _():
        cost_copy(0).wait_send()

    for dx in (2, 1, 3):
        cost_copy(dx).wait_send()
        spread_copy(dx).wait_send()
    for dx in range(4):
        spread_hand(dx, c).wait_send()
    out_pg.wait()
    out_pc.wait()
    out_sp.wait()


def finish(po, sw, nz, pcr, pgr, spr, pc, pg, ch):
    c, y, z, x = place()
    zlane = pl.ds(pl.multiple_of(z * 128, 128), 128)
    diag = lax.broadcasted_iota(jnp.int32, (32, 128), 1) == (
        32 * x + lax.broadcasted_iota(jnp.int32, (32, 128), 0)
    )
    pick = lax.broadcasted_iota(jnp.int32, (32, 32), 1) == lax.broadcasted_iota(jnp.int32, (32, 32), 0)

    def on_diag(row):
        column = jnp.sum(jnp.where(pick, row, 0.0), axis=1, keepdims=True)
        return jnp.where(diag, column, 0.0).reshape(2, 16, 128)

    pg[...] = pgr[...]
    pc[...] = pcr[...]
    for j in range(2):
        pc[j, :, :, zlane] += on_diag(sw[j : j + 1, :])
    for k in range(8):
        parent = [po[k] == 4 * y + q for q in range(4)]

        def fill(i, _):
            cols = pl.ds(pl.multiple_of(i * 256, 256), 256)
            v = spr[0, :, :, cols]
            for q in range(1, 4):
                v = jnp.where(parent[q], spr[q, :, :, cols], v)
            ch[k, :, :, cols] = v
            return 0

        lax.fori_loop(0, 4, fill, 0)
        ch[k, :, :, zlane] += on_diag(nz[k : k + 1, :])


def on_device(cc, cw, po, a, b, sw, iw, pcov, nz):
    any_, vmem, smem = (pl.BlockSpec(memory_space=m) for m in (pl.ANY, pltpu.VMEM, pltpu.SMEM))
    v, dma = pltpu.VMEM, pltpu.SemaphoreType.DMA
    scratch = [
        v((8, 32, 1024), F32),
        v((8, 4, 2, 16, 1024), BF16),
        v((8, 4, 2, 16, 256), BF16),
        v((8, 4, 2, 16, 1024), BF16),
        v((320, 1536), BF16),
        v((8, 4, 2, 16, 128 * BLOCKS + 128), BF16),
        v((8, 4, 2, 16, 128 * BLOCKS), BF16),
        v((320, 1024), F32),
        v((4, 2, 16, 1024), F32),
        v((4, 16, 1024), F32),
        v((8, 128), F32),
        v((8, 128), F32),
        v((2, 256), F32),
        v((2, 256), F32),
        v((2, 32, 1024), BF16),
        v((2, 32, 128 * BLOCKS), BF16),
        v((4, 16, 128 * BLOCKS + 128), BF16),
        v((320, 1024), BF16),
        v((320, 1024), BF16),
        v((320, 1024), F32),
        v((256, 1024), F32),
        v((256, 1024), BF16),
        v((256, 1024), BF16),
        v((64, 1536), BF16),
        v((64, 1024), F32),
        v((4, 16, 1024), F32),
        v((2, 2, 16, 1024), F32),
        v((2, 8, 1024), F32),
        v((4, 16, 1024), F32),
        v((4, 2, 16, 1024), F32),
        dma((5,)), dma((1,)), dma((3,)),
        dma((3,)), dma((3,)),
        dma((4,)), dma((4,)),
        dma((4, 2)), dma((4,)),
        dma((2, 4, 4)), dma((2, 4, 4)), dma((2, 5, 4)), dma((2, 5, 4)),
        dma((2, 4, 4)), dma((2, 4, 4)), dma((2, 5, 4)), dma((2, 5, 4)),
        dma((4,)), dma((4,)),
        dma((4,)), dma((4, 2)),
        dma((4,)), dma((4,)), dma((4,)), dma((4,)),
    ]
    pcr, pgr, spr = pl.pallas_call(
        kernel,
        out_shape=(
            jax.ShapeDtypeStruct((2, 2, 16, 1024), F32),
            jax.ShapeDtypeStruct((2, 8, 1024), F32),
            jax.ShapeDtypeStruct((4, 2, 16, 1024), F32),
        ),
        in_specs=[smem, smem, any_, any_, any_, any_, any_],
        out_specs=(any_, any_, any_),
        scratch_shapes=scratch,
        compiler_params=pltpu.CompilerParams(collective_id=0, has_side_effects=True),
    )(cw, po, cc, a.reshape(8, 4, 2, 16, 1024), b.reshape(8, 4, 2, 16, 256), iw, pcov)
    pc, pg, ch = pl.pallas_call(
        finish,
        out_shape=(
            jax.ShapeDtypeStruct((2, 2, 16, 1024), F32),
            jax.ShapeDtypeStruct((2, 8, 1024), F32),
            jax.ShapeDtypeStruct((8, 2, 16, 1024), F32),
        ),
        in_specs=[smem] + [vmem] * 5,
        out_specs=(vmem, vmem, vmem),
    )(po, sw, nz, pcr, pgr, spr)
    return pc.reshape(2, 32, 1024), pg, ch.reshape(8, 32, 1024)


def solution(mesh):
    rows = P("node", "tile", None)
    placed = (rows, P("node"), P("node"), P(), P(), P("node", "tile"), P("node", None), rows, P("node", "tile"))
    return jax.shard_map(
        on_device, mesh=mesh, in_specs=placed, out_specs=(rows, rows, rows), check_vma=False
    )
```

time: 78.1 us -> 69.1 us (0.88)
  local copies, waits for them, and re-layouts: 5.45 us -> 0 us
  Pallas kernels: 71.7 us -> 68.3 us
    pallas_call x1, Pallas kernels: 71.7 us -> 65.1 us  [on_device(): pl.pallas_call(kernel, out_shape=(jax.ShapeDtypeStruct((2, 2, 16, 1024),...]
    unnamed x3 -> x0, local copies, waits for them, and re-layouts: 5.45 us -> none
    pallas_call x0 -> x1, Pallas kernels: none -> 3.26 us  [on_device(): pl.pallas_call(finish, out_shape=(jax.ShapeDtypeStruct((2, 2, 16, 1024),...]
where the time goes in v1:
time: 69.1 us; the launch traced here: 69 us
  Pallas kernels  68.3 us (99%)
    pallas_call x1, Pallas kernels, on_device(): pl.pallas_call(kernel, out_shape=(jax.ShapeDtypeStruct((2, 2, 16, 1024),...  65.1 us
    pallas_call x1, Pallas kernels, on_device(): pl.pallas_call(finish, out_shape=(jax.ShapeDtypeStruct((2, 2, 16, 1024),...  3.26 us

profile of v1, /device:TPU:1, one launch (start us, length us, event | category | flops | bytes accessed | tf_op | source)
XLA Modules:
  0.0 69.0 jit_solution(10425439256383597272)
XLA Ops:
  0.6 65.1 %shard_map.112 = (f32[2,2,16,1024]{3,2,1,0:T(8,128)}, f32[2,8,1024]{2,1,0:T(8,128)}, f32[4,2,16,1024]{3,2,1,0:T(8,128)}) custom-call(s32[8]{0:T(128)} %cw.1, s32[8]{0:T(128)} %po.3, f32[8,32,1024]{2,1,0:T(8,128)} %cc.1, bf16[8,4,2,16,1024]{4,3,2,1,0:T(8,128)(2,1)} %bitcast.4, bf16[8,4,2,16,256]{4,3,2,1,0:T(8,128)(2,1)} %bitcast.5, f32[2,256]{1,0:T(2,128)} %iw_in.1, ...), custom_call_target="tpu_custom_call" | custom-call | tf_op jit(solution)/shard_map/pallas_call | solution.py:585
  65.7 3.3 %shard_map.113 = (f32[2,2,16,1024]{3,2,1,0:T(8,128)}, f32[2,8,1024]{2,1,0:T(8,128)}, f32[8,2,16,1024]{3,2,1,0:T(8,128)}) custom-call(s32[8]{0:T(128)} %po.3, f32[2,32]{1,0:T(2,128)} %sw.1, f32[8,32]{1,0:T(8,128)} %nz.1, f32[2,2,16,1024]{3,2,1,0:T(8,128)} %get-tuple-element.9.pcr, f32[2,8,1024]{2,1,0:T(8,128)} %get-tuple-element.10.pgr, ...), custom_call_target="tpu_custom_call" | custom-call | tf_op jit(solution)/shard_map/pallas_call | solution.py:597

commit v2 on v1

--- a/solution.py
+++ b/solution.py
@@ -64,7 +64,7 @@
     return out
 
 
-def sweep(a, trips, beside=None, b=4, unroll=8):
+def sweep(a, trips, beside=None, b=4, unroll=32):
     n = a.shape[0]
     lane = lax.broadcasted_iota(jnp.int32, (1, n), 1)
     lanes = lax.broadcasted_iota(jnp.int32, (n, n), 1)
@@ -97,6 +97,7 @@
 
 ORDER = (0, 1, 3, 2)
 HOPS = ((4, 3, 3, 4), (3, 4, 4, 3))
+NEAR = (1, -1, 2, -2, 3, -3)
 BLOCKS = 5
 
 
@@ -106,13 +107,13 @@
 
 
 def kernel(
-    cw, po, cc, a_in, b_in, iw_in, pcov_in,
+    cw_in, po_in, cc, a_in, b_in, iw_in, pcov_in,
     pcr_out, pgr_out, spr_out,
     ccv, a5, b5, at5, lt, e5, p5, acc, mine, theirs, wt, wr, iw, iwr, pcov, pk, eb,
-    bh, bl, cpl, gv, gh, gl, cl2, mom, pcv, pcr, pgr, spv, spr,
+    bh, bl, cpl, gv, gh, gl, cl2, mom, pcv, pcr, pgr, spv, spr, cost_via, spread_via, cw, po,
     load_sem, loc_sem, out_sem, sa_s, sa_r, sb_s, sb_r, pa_s, pa_r,
-    er_s, er_r, ef_s, ef_r, pr_s, pr_r, pf_s, pf_r,
-    gs_s, gs_r, cs_s, cs_r, ss_s, ss_r, sf_s, sf_r,
+    er_s, er_r, ef_s, ef_r, pr_s, pr_r, pf_s, pf_r, far_s, far_r,
+    gs_s, gs_r, cs_s, cs_r, ss_s, ss_r, sf_s, sf_r, via_s, via_r, on_s,
 ):
     c, y, z, x = place()
     oc = 1 - c
@@ -140,7 +141,7 @@
     for dx in range(4):
         for core in ((oc,) if dx == 0 else (c, oc)):
             pl.semaphore_signal(barrier, inc=1, device_id=dev(core, z, xs(dx)), device_id_type=MESH)
-    for dz in (1, -1):
+    for dz in range(1, 8):
         pl.semaphore_signal(barrier, inc=1, device_id=dev(c, zs(dz), x), device_id_type=MESH)
 
     loads = [
@@ -149,9 +150,13 @@
         pltpu.make_async_copy(a_in, a5, load_sem.at[2]),
         pltpu.make_async_copy(iw_in, iw, load_sem.at[3]),
         pltpu.make_async_copy(pcov_in, pcov, load_sem.at[4]),
+        pltpu.make_async_copy(cw_in, cw, load_sem.at[5]),
+        pltpu.make_async_copy(po_in, po, load_sem.at[6]),
     ]
-    for cp in loads:
-        cp.start()
+    for i in (5, 6, 0, 1, 2, 3, 4):
+        loads[i].start()
+    loads[5].wait()
+    loads[6].wait()
 
     first = 4 * y
     coef = [
@@ -183,7 +188,7 @@
     lax.fori_loop(0, 4, weigh, 0)
 
     loads[3].wait()
-    pl.semaphore_wait(barrier, 9)
+    pl.semaphore_wait(barrier, 14)
 
     pair = dev(oc, z, x)
     swap = [
@@ -193,22 +198,6 @@
     ]
     for cp in swap:
         cp.start()
-
-    loads[1].wait()
-    lt[0:256, 0:1024] = b5[...].reshape(1024, 256).T
-    loads[2].wait()
-
-    def turn(i, _):
-        block = a5[pl.ds(i, 1)].reshape(128, 1024)
-        at5[:, :, :, :, pl.ds(pl.multiple_of(i * 128, 128), 128)] = block.T.reshape(8, 4, 2, 16, 128)
-        return 0
-
-    lax.fori_loop(0, 8, turn, 0)
-    lt[256:320, 0:1024] = at5[z, :, c].reshape(64, 1024)
-    lt[:, 1024:1536] = lt[:, 0:512]
-    loads[4].wait()
-    for p in range(BLOCKS):
-        pk[:, :, 128 * p : 128 * p + 128] = pcov[:, :, lanes(z + p)]
 
     for cp in swap:
         cp.wait_recv()
@@ -301,7 +290,32 @@
                     hand(buf, fs, fr, d, s, h, c).wait_send()
 
     e_ring = (e5, er_s, er_r, ef_s, ef_r)
-    p_ring = (p5, pr_s, pr_r, pf_s, pf_r)
+
+    def cov_send(dz):
+        part = p5.at[z, :, c]
+        return remote(part, part, pr_s.at[dz + 3], pr_r.at[dz + 3], dev(c, zs(dz), x))
+
+    def cov_got(dz):
+        part = p5.at[zs(-dz), :, c]
+        return remote(part, part, pr_s.at[dz + 3], pr_r.at[dz + 3], pair)
+
+    def cov_hand(dz, core):
+        part = p5.at[zs(-dz), :, core]
+        return remote(part, part, pf_s.at[dz + 3], pf_r.at[dz + 3], pair)
+
+    def cov_onward(d, got=False):
+        sign = 1 - 2 * d
+        part = p5.at[zs(4 if got else -3 * sign), pl.ds(2 * d, 2), c]
+        return remote(part, part, far_s.at[d], far_r.at[d], dev(c, zs(sign), x))
+
+    def cov_far_hand(d, core):
+        part = p5.at[zs(4), pl.ds(2 * d, 2), core]
+        return remote(part, part, far_s.at[2 + d], far_r.at[2 + d], pair)
+
+    def cov_take(dz):
+        cov_got(dz).wait_recv()
+        cov_hand(dz, c).start()
+
 
     def chunk_add(buf, zc, left2, out):
         left = left2[:, lanes(zc)]
@@ -315,21 +329,45 @@
         out[:, lanes(zc)] += mm(turned, chunk[:, 128:512], ((1,), (1,)))
 
     ring_start(*e_ring, 0)
+    loads[1].wait()
+    lt[0:256, 0:1024] = b5[...].reshape(1024, 256).T
+    loads[2].wait()
+
+    def turn(i, _):
+        block = a5[pl.ds(i, 1)].reshape(128, 1024)
+        at5[:, :, :, :, pl.ds(pl.multiple_of(i * 128, 128), 128)] = block.T.reshape(8, 4, 2, 16, 128)
+        return 0
+
+    lax.fori_loop(0, 8, turn, 0)
+    lt[256:320, 0:1024] = at5[z, :, c].reshape(64, 1024)
+    lt[:, 1024:1536] = lt[:, 0:512]
+    loads[4].wait()
+    for p in range(BLOCKS):
+        pk[:, :, 128 * p : 128 * p + 128] = pcov[:, :, lanes(z + p)]
     acc[...] = jnp.zeros_like(acc)
     for dx in ORDER[1:]:
         remote(eb.at[xs(dx)], e5.at[z, xs(-dx), c], sb_s.at[dx], sb_r.at[dx], dev(c, z, xs(dx))).wait_recv()
         ring_start(*e_ring, dx)
     cov_start()
-    for s in range(1, 5):
-        ring_step(*e_ring, s, ORDER[:2])
-        hand_wait(e5, ef_s, ef_r, s - 1)
-        chunk_add(e5, zs(1 - s), lt, acc)
-        ring_step(*e_ring, s, ORDER[2:])
-        if s > 1:
-            chunk_add(e5, zs(s - 1), lt, acc)
+    ring_step(*e_ring, 1)
+    hand_wait(e5, ef_s, ef_r, 0)
+    chunk_add(e5, z, lt, acc)
+    ring_step(*e_ring, 2)
+    hand_wait(e5, ef_s, ef_r, 1)
+    chunk_add(e5, zs(1), lt, acc)
+    ring_step(*e_ring, 3)
+    chunk_add(e5, zs(-1), lt, acc)
+    hand_wait(e5, ef_s, ef_r, 2)
+    chunk_add(e5, zs(2), lt, acc)
+    chunk_add(e5, zs(-2), lt, acc)
+    ring_step(*e_ring, 4)
     cov_wait()
-    for h in ORDER:
-        ring_start(*p_ring, h)
+    cov_hand(0, c).start()
+    for dz in NEAR:
+        cov_send(dz).start()
+    hand_wait(e5, ef_s, ef_r, 3)
+    chunk_add(e5, zs(3), lt, acc)
+    chunk_add(e5, zs(-3), lt, acc)
     hand_wait(e5, ef_s, ef_r, 4)
     chunk_add(e5, zs(4), lt, acc)
 
@@ -345,23 +383,25 @@
     cpl_own = split(small[256:320])
 
     def times_a(trip):
-        rows = pl.ds(pl.multiple_of(lax.rem(trip, 2) * 160, 32), 160)
-        cols = pl.ds(pl.multiple_of((trip // 2) * 256, 256), 256)
-        right = a5[:, :, :, :, cols].reshape(1024, 256)
-        cpl[rows, cols] = mm(bh[rows, :], right) + mm(bl[rows, :], right)
+        for part in range(2):
+            cols = pl.ds(pl.multiple_of(trip * 512 + part * 256, 256), 256)
+            right = a5[:, :, :, :, cols].reshape(1024, 256)
+            cpl[:, cols] = mm(bh[...], right) + mm(bl[...], right)
 
     s11, s12, s22 = curv[:128, :128], curv[:128, 128:], curv[128:, 128:]
-    inv = sweep(s11, 8, times_a)
-    ring_step(*p_ring, 1)
-    inv = sweep(inv, 8)
-    ring_step(*p_ring, 2)
+    inv = sweep(s11, 2, times_a)
+    inv = sweep(inv, 2)
+    cov_take(1)
+    cov_take(-1)
     inv_s, s12_s = split(inv), split(s12)
     w = mm3(inv_s, s12_s)
     w_s = split(w)
-    inv2 = sweep(s22 - mm3(s12_s, w_s, ((0,), (0,))), 8)
-    ring_step(*p_ring, 3)
-    inv2 = sweep(inv2, 8)
-    ring_step(*p_ring, 4)
+    inv2 = sweep(s22 - mm3(s12_s, w_s, ((0,), (0,))), 2)
+    for dz in (2, -2, 3, -3):
+        cov_take(dz)
+    for d in range(2):
+        cov_onward(d).start()
+    inv2 = sweep(inv2, 2)
     wq = mm3(w_s, split(inv2))
     inv1 = inv + mm3(split(wq), w_s, ((1,), (1,)))
     full_s = split(
@@ -379,6 +419,10 @@
 
     lax.fori_loop(0, 4, back, 0)
 
+    for d in range(2):
+        cov_onward(d, True).wait_recv()
+        cov_far_hand(d, c).start()
+
     def gain_copy(dx):
         xx = xs(dx)
         rows = pl.ds(pl.multiple_of(32 * z + 8 * xx, 8), 8)
@@ -401,7 +445,19 @@
     def cost_copy(dx):
         return remote(pcv.at[xs(dx)], pcr.at[jq, c], cs_s.at[dx], cs_r.at[dx, c], dev(own, z, xs(dx)))
 
-    for dx in (2, 1, 3):
+    way = 1 - 2 * c
+    source = xs(-way)
+
+    def cost_near():
+        return remote(pcv.at[xs(2)], cost_via, via_s.at[0], via_r.at[0], dev(c, z, xs(way)))
+
+    def cost_onward():
+        return remote(
+            cost_via, pcr.at[lax.rem(source, 2), c], on_s.at[0], cs_r.at[2, c], dev(source // 2, z, xs(way))
+        )
+
+    cost_near().start()
+    for dx in (1, 3):
         cost_copy(dx).start()
 
     @pl.when(own == c)
@@ -417,65 +473,73 @@
     closed = (a_rows - (mm(b_rows, gh[...]) + mm(b_rows, gl[...]))).astype(BF16)
     cl2[:, 0:1024] = closed
     cl2[:, 1024:1536] = closed[:, 0:512]
-    mom[...] = jnp.zeros_like(mom)
-    for s in range(5):
-        hand_wait(p5, pf_s, pf_r, s)
-
-    def moment(i, _):
-        chunk_add(p5, i, cl2, mom)
-        return 0
-
-    lax.fori_loop(0, 8, moment, 0)
+    for dz in (0,) + NEAR:
+        cov_hand(dz, oc).wait_recv()
+    for d in range(2):
+        cov_far_hand(d, oc).wait_recv()
+    nt = ((1,), (1,))
+    for q in range(8):
+        low = (q - BLOCKS + 1) % 8
+        right = jnp.concatenate(
+            [
+                p5[(low + i) % 8, :, :, :, 128 * (BLOCKS - 1 - i) : 128 * (BLOCKS - i)].reshape(128, 128)
+                for i in range(BLOCKS)
+            ],
+            axis=0,
+        )
+        mom[:, 128 * q : 128 * q + 128] = mm(cl2[:, 128 * low : 128 * (low + BLOCKS)], right) + mm(
+            cl2[:, 128 * (q + 1) : 128 * (q + 4)], p5[q, :, :, :, 128:512].reshape(128, 384), nt
+        )
     moment_s = split(mom[...])
-    nt = ((1,), (1,))
     inner_s = split(mm3(moment_s, (gh[...], gl[...]), nt))
 
-    def out_cols(i, _):
-        cols = pl.ds(pl.multiple_of(i * 256, 256), 256)
-        v = mm2(moment_s, at5[:, :, :, :, cols].reshape(1024, 256)) - mm2(inner_s, lt[0:256, cols])
-        spv[:, :, cols] = v.reshape(4, 16, 256)
-        return 0
-
-    lax.fori_loop(0, 4, out_cols, 0)
-
-    def spread_copy(dx):
-        return remote(spv.at[xs(dx)], spr.at[x, c], ss_s.at[dx], ss_r.at[dx], dev(c, z, xs(dx)))
-
-    def spread_got(dx):
-        return remote(spv.at[xs(dx)], spr.at[xs(-dx), c], ss_s.at[dx], ss_r.at[dx], dev(c, z, xs(dx)))
-
-    def spread_hand(dx, core):
-        return remote(spr.at[xs(-dx), core], spr.at[xs(-dx), core], sf_s.at[dx], sf_r.at[dx], pair)
-
-    for dx in (2, 1, 3):
-        spread_copy(dx).start()
-    spr[x, c] = spv[x]
-    spread_hand(0, c).start()
-
-    for dx in (1, 2, 3):
-        @pl.when(xs(-dx) // 2 == c)
-        def _(dx=dx):
-            remote(gv.at[0:8], pgr.at[lax.rem(xs(-dx), 2)], gs_s.at[dx], gs_r.at[dx], pair).wait_recv()
-            for core in range(2):
-                remote(pcv.at[0], pcr.at[lax.rem(xs(-dx), 2), core], cs_s.at[dx], cs_r.at[dx, core], pair).wait_recv()
-
-    @pl.when(own == c)
-    def _():
-        remote(pcv.at[0], pcr.at[jq, oc], cs_s.at[0], cs_r.at[0, oc], pair).wait_recv()
-
-    out_pg = pltpu.make_async_copy(pgr, pgr_out, out_sem.at[0])
-    out_pg.start()
-    out_pc = pltpu.make_async_copy(pcr, pcr_out, out_sem.at[1])
-    out_pc.start()
-
-    for dx in (1, 3, 2):
-        spread_got(dx).wait_recv()
-        spread_hand(dx, c).start()
-    for dx in range(4):
-        spread_hand(dx, oc).wait_recv()
-
-    out_sp = pltpu.make_async_copy(spr, spr_out, out_sem.at[2])
-    out_sp.start()
+    cost_near().wait_recv()
+    cost_onward().start()
+
+    def spread_copy(dx, half):
+        cols = pl.ds(512 * half, 512)
+        return remote(
+            spv.at[xs(dx), :, cols], spr.at[x, c, :, cols], ss_s.at[dx, half], ss_r.at[dx, half], dev(c, z, xs(dx))
+        )
+
+    def spread_got(dx, half):
+        cols = pl.ds(512 * half, 512)
+        return remote(
+            spv.at[xs(dx), :, cols], spr.at[xs(-dx), c, :, cols], ss_s.at[dx, half], ss_r.at[dx, half], dev(c, z, xs(dx))
+        )
+
+    def spread_hand(dx, half, core):
+        part = spr.at[xs(-dx), core, :, pl.ds(512 * half, 512)]
+        return remote(part, part, sf_s.at[dx, half], sf_r.at[dx, half], pair)
+
+    def spread_near(half):
+        return remote(
+            spv.at[xs(2), :, pl.ds(512 * half, 512)], spread_via.at[half],
+            via_s.at[1 + half], via_r.at[1 + half], dev(c, z, xs(way)),
+        )
+
+    def spread_onward(half):
+        return remote(
+            spread_via.at[half], spr.at[source, c, :, pl.ds(512 * half, 512)],
+            on_s.at[1 + half], ss_r.at[2, half], dev(c, z, xs(way)),
+        )
+
+    for half in range(2):
+        for i in range(2):
+            cols = slice(512 * half + 256 * i, 512 * half + 256 * i + 256)
+            v = mm2(moment_s, at5[:, :, :, :, cols].reshape(1024, 256)) - mm2(inner_s, lt[0:256, cols])
+            spv[:, :, cols] = v.reshape(4, 16, 256)
+
+        spread_near(half).start()
+        for dx in (1, 3):
+            spread_copy(dx, half).start()
+        cols = slice(512 * half, 512 * half + 512)
+        spr[x, c, :, cols] = spv[x, :, cols]
+        spread_hand(0, half, c).start()
+
+    for half in range(2):
+        spread_near(half).wait_recv()
+        spread_onward(half).start()
 
     for cp in swap + spread_e:
         cp.wait_send()
@@ -486,7 +550,41 @@
             if dx:
                 cov_copy(dx, False).wait_send()
     drain(*e_ring)
-    drain(*p_ring)
+    cov_hand(0, c).wait_send()
+    for dz in NEAR:
+        cov_send(dz).wait_send()
+        cov_hand(dz, c).wait_send()
+    for d in range(2):
+        cov_onward(d).wait_send()
+        cov_far_hand(d, c).wait_send()
+
+    for dx in (1, 2, 3):
+        @pl.when(xs(-dx) // 2 == c)
+        def _(dx=dx):
+            remote(gv.at[0:8], pgr.at[lax.rem(xs(-dx), 2)], gs_s.at[dx], gs_r.at[dx], pair).wait_recv()
+            for core in range(2):
+                remote(pcv.at[0], pcr.at[lax.rem(xs(-dx), 2), core], cs_s.at[dx], cs_r.at[dx, core], pair).wait_recv()
+
+    @pl.when(own == c)
+    def _():
+        remote(pcv.at[0], pcr.at[jq, oc], cs_s.at[0], cs_r.at[0, oc], pair).wait_recv()
+
+    out_pg = pltpu.make_async_copy(pgr, pgr_out, out_sem.at[0])
+    out_pg.start()
+    out_pc = pltpu.make_async_copy(pcr, pcr_out, out_sem.at[1])
+    out_pc.start()
+
+    for half in range(2):
+        for dx in (1, 3, 2):
+            spread_got(dx, half).wait_recv()
+            spread_hand(dx, half, c).start()
+    out_own = pltpu.make_async_copy(spr.at[:, c], spr_out.at[:, c], out_sem.at[2])
+    out_own.start()
+    for half in range(2):
+        for dx in range(4):
+            spread_hand(dx, half, oc).wait_recv()
+    out_pair = pltpu.make_async_copy(spr.at[:, oc], spr_out.at[:, oc], out_sem.at[3])
+    out_pair.start()
 
     @pl.when(own == c)
     def _():
@@ -497,17 +595,29 @@
     def _():
         cost_copy(0).wait_send()
 
-    for dx in (2, 1, 3):
+    cost_near().wait_send()
+    cost_onward().wait_send()
+    for half in range(2):
+        spread_near(half).wait_send()
+        spread_onward(half).wait_send()
+    for dx in (1, 3):
         cost_copy(dx).wait_send()
-        spread_copy(dx).wait_send()
-    for dx in range(4):
-        spread_hand(dx, c).wait_send()
+        for half in range(2):
+            spread_copy(dx, half).wait_send()
+    for half in range(2):
+        for dx in range(4):
+            spread_hand(dx, half, c).wait_send()
     out_pg.wait()
     out_pc.wait()
-    out_sp.wait()
-
-
-def finish(po, sw, nz, pcr, pgr, spr, pc, pg, ch):
+    out_own.wait()
+    out_pair.wait()
+
+
+def finish(po, sw, nz, pcr, pgr, spr, pc_out, pg_out, ch_out, pc, pg, ch, out_sem):
+    outs = [
+        pltpu.make_async_copy(pg, pg_out, out_sem.at[8]),
+        pltpu.make_async_copy(pc, pc_out, out_sem.at[9]),
+    ]
     c, y, z, x = place()
     zlane = pl.ds(pl.multiple_of(z * 128, 128), 128)
     diag = lax.broadcasted_iota(jnp.int32, (32, 128), 1) == (
@@ -519,10 +629,6 @@
         column = jnp.sum(jnp.where(pick, row, 0.0), axis=1, keepdims=True)
         return jnp.where(diag, column, 0.0).reshape(2, 16, 128)
 
-    pg[...] = pgr[...]
-    pc[...] = pcr[...]
-    for j in range(2):
-        pc[j, :, :, zlane] += on_diag(sw[j : j + 1, :])
     for k in range(8):
         parent = [po[k] == 4 * y + q for q in range(4)]
 
@@ -536,6 +642,17 @@
 
         lax.fori_loop(0, 4, fill, 0)
         ch[k, :, :, zlane] += on_diag(nz[k : k + 1, :])
+        outs.append(pltpu.make_async_copy(ch.at[k], ch_out.at[k], out_sem.at[k]))
+        outs[-1].start()
+        if k == 1:
+            pg[...] = pgr[...]
+            outs[0].start()
+            pc[...] = pcr[...]
+            for j in range(2):
+                pc[j, :, :, zlane] += on_diag(sw[j : j + 1, :])
+            outs[1].start()
+    for cp in outs:
+        cp.wait()
 
 
 def on_device(cc, cw, po, a, b, sw, iw, pcov, nz):
@@ -572,24 +689,24 @@
         v((2, 8, 1024), F32),
         v((4, 16, 1024), F32),
         v((4, 2, 16, 1024), F32),
-        dma((5,)), dma((1,)), dma((3,)),
+        v((16, 1024), F32),
+        v((2, 16, 512), F32),
+        pltpu.SMEM((8,), jnp.int32), pltpu.SMEM((8,), jnp.int32),
+        dma((7,)), dma((1,)), dma((4,)),
         dma((3,)), dma((3,)),
         dma((4,)), dma((4,)),
         dma((4, 2)), dma((4,)),
         dma((2, 4, 4)), dma((2, 4, 4)), dma((2, 5, 4)), dma((2, 5, 4)),
-        dma((2, 4, 4)), dma((2, 4, 4)), dma((2, 5, 4)), dma((2, 5, 4)),
+        dma((7,)), dma((7,)), dma((7,)), dma((7,)), dma((4,)), dma((4,)),
         dma((4,)), dma((4,)),
         dma((4,)), dma((4, 2)),
-        dma((4,)), dma((4,)), dma((4,)), dma((4,)),
+        dma((4, 2)), dma((4, 2)), dma((4, 2)), dma((4, 2)),
+        dma((3,)), dma((3,)), dma((3,)),
     ]
     pcr, pgr, spr = pl.pallas_call(
         kernel,
-        out_shape=(
-            jax.ShapeDtypeStruct((2, 2, 16, 1024), F32),
-            jax.ShapeDtypeStruct((2, 8, 1024), F32),
-            jax.ShapeDtypeStruct((4, 2, 16, 1024), F32),
-        ),
-        in_specs=[smem, smem, any_, any_, any_, any_, any_],
+        out_shape=(v((2, 2, 16, 1024), F32), v((2, 8, 1024), F32), v((4, 2, 16, 1024), F32)),
+        in_specs=[any_] * 7,
         out_specs=(any_, any_, any_),
         scratch_shapes=scratch,
         compiler_params=pltpu.CompilerParams(collective_id=0, has_side_effects=True),
@@ -602,7 +719,11 @@
             jax.ShapeDtypeStruct((8, 2, 16, 1024), F32),
         ),
         in_specs=[smem] + [vmem] * 5,
-        out_specs=(vmem, vmem, vmem),
+        out_specs=(any_, any_, any_),
+        scratch_shapes=[
+            v((2, 2, 16, 1024), F32), v((2, 8, 1024), F32), v((8, 2, 16, 1024), F32), dma((10,)),
+        ],
+        compiler_params=pltpu.CompilerParams(vmem_limit_bytes=8 * 2**20),
     )(po, sw, nz, pcr, pgr, spr)
     return pc.reshape(2, 32, 1024), pg, ch.reshape(8, 32, 1024)
 

time: 69.1 us -> 64.7 us (0.936)
  Pallas kernels: 68.3 us -> 63.9 us
    pallas_call x1, Pallas kernels: 65.1 us -> 61.6 us  [on_device(): pl.pallas_call(kernel, out_shape=(v((2, 2, 16, 1024), F32), v((2, 8, 1024...]
    pallas_call x1, Pallas kernels: 3.26 us -> 2.3 us  [on_device(): pl.pallas_call(finish, out_shape=(jax.ShapeDtypeStruct((2, 2, 16, 1024),...]
where the time goes in v2:
time: 64.7 us; the launch traced here: 64.6 us
  Pallas kernels  63.9 us (99%)
  between operations  0.69 us (1%)
    pallas_call x1, Pallas kernels, on_device(): pl.pallas_call(kernel, out_shape=(v((2, 2, 16, 1024), F32), v((2, 8, 1024...  61.6 us
    pallas_call x1, Pallas kernels, on_device(): pl.pallas_call(finish, out_shape=(jax.ShapeDtypeStruct((2, 2, 16, 1024),...  2.3 us

profile of v2, /device:TPU:1, one launch (start us, length us, event | category | flops | bytes accessed | tf_op | source)
XLA Modules:
  0.0 64.6 jit_solution(15490991101335339527)
XLA Ops:
  0.6 0.0 copy-start.1
  0.6 0.0 copy-start
  0.7 0.0 copy-start.2
  0.7 61.6 %shard_map.112 = (f32[2,2,16,1024]{3,2,1,0:T(8,128)S(1)}, f32[2,8,1024]{2,1,0:T(8,128)S(1)}, f32[4,2,16,1024]{3,2,1,0:T(8,128)S(1)}) custom-call(s32[8]{0:T(128)} %cw_in.1, s32[8]{0:T(128)} %po.1, f32[8,32,1024]{2,1,0:T(8,128)} %cc.1, bf16[8,4,2,16,1024]{4,3,2,1,0:T(8,128)(2,1)} %bitcast.4, bf16[8,4,2,16,256]{4,3,2,1,0:T(8,128)(2,1)} %bitcast.5, ...), custom_call_target="tpu_custom_call" | custom-call | tf_op jit(solution)/shard_map/pallas_call | solution.py:706
  62.3 0.0 copy-done.1
  62.3 0.0 copy-done
  62.3 0.0 copy-done.2
  62.3 2.3 %shard_map.113 = (f32[2,2,16,1024]{3,2,1,0:T(8,128)}, f32[2,8,1024]{2,1,0:T(8,128)}, f32[8,2,16,1024]{3,2,1,0:T(8,128)}) custom-call(s32[8]{0:T(128)S(1)} %copy-done.1, f32[2,32]{1,0:T(2,128)S(1)} %copy-done.2, f32[8,32]{1,0:T(8,128)S(1)} %copy-done, f32[2,2,16,1024]{3,2,1,0:T(8,128)S(1)} %get-tuple-element.9.pcr, f32[2,8,1024]{2,1,0:T(8,128)S(1)} %get-tuple-element.10.pgr, ...), custom_call_target="tpu_custom_call" | custom-call | tf_op jit(solution)/shard_map/pallas_call | solution.py:714
Async XLA Ops:
  0.6 61.6 %copy-start.1 = (s32[8]{0:T(128)S(1)}, s32[8]{0:T(128)}, u32[]{:S(2)}) copy-start(s32[8]{0:T(128)} %po.1) | copy-start | bytes 100
  0.6 61.6 %copy-start = (f32[8,32]{1,0:T(8,128)S(1)}, f32[8,32]{1,0:T(8,128)}, u32[]{:S(2)}) copy-start(f32[8,32]{1,0:T(8,128)} %nz.1) | copy-start | bytes 3076
  0.7 61.6 %copy-start.2 = (f32[2,32]{1,0:T(2,128)S(1)}, f32[2,32]{1,0:T(2,128)}, u32[]{:S(2)}) copy-start(f32[2,32]{1,0:T(2,128)} %sw.1) | copy-start | bytes 772

commit v3 on v2

--- a/solution.py
+++ b/solution.py
@@ -21,11 +21,15 @@
 
 
 def mm2(a, b, dims=((1,), (0,))):
-    return mm(a[0], b, dims) + mm(a[1], b, dims)
+    m = a[0].shape[0]
+    r = mm(jnp.concatenate(a, axis=0), b, dims)
+    return r[:m] + r[m:]
 
 
 def mm3(a, b, dims=((1,), (0,))):
-    return mm(a[0], b[0], dims) + (mm(a[0], b[1], dims) + mm(a[1], b[0], dims))
+    if dims[0] == (0,):
+        return mm(a[0], b[0], dims) + (mm(a[0], b[1], dims) + mm(a[1], b[0], dims))
+    return mm2(a, b[0], dims) + mm(a[0], b[1], dims)
 
 
 def total(terms):
@@ -141,7 +145,7 @@
     for dx in range(4):
         for core in ((oc,) if dx == 0 else (c, oc)):
             pl.semaphore_signal(barrier, inc=1, device_id=dev(core, z, xs(dx)), device_id_type=MESH)
-    for dz in range(1, 8):
+    for dz in (1, -1, 2, -2):
         pl.semaphore_signal(barrier, inc=1, device_id=dev(c, zs(dz), x), device_id_type=MESH)
 
     loads = [
@@ -188,7 +192,7 @@
     lax.fori_loop(0, 4, weigh, 0)
 
     loads[3].wait()
-    pl.semaphore_wait(barrier, 14)
+    pl.semaphore_wait(barrier, 11)
 
     pair = dev(oc, z, x)
     swap = [
@@ -292,8 +296,12 @@
     e_ring = (e5, er_s, er_r, ef_s, ef_r)
 
     def cov_send(dz):
-        part = p5.at[z, :, c]
-        return remote(part, part, pr_s.at[dz + 3], pr_r.at[dz + 3], dev(c, zs(dz), x))
+        if abs(dz) == 3:
+            held, hop = zs(-2 * dz // 3), dz // 3
+        else:
+            held, hop = z, dz
+        part = p5.at[held, :, c]
+        return remote(part, part, pr_s.at[dz + 3], pr_r.at[dz + 3], dev(c, zs(hop), x))
 
     def cov_got(dz):
         part = p5.at[zs(-dz), :, c]
@@ -363,7 +371,7 @@
     ring_step(*e_ring, 4)
     cov_wait()
     cov_hand(0, c).start()
-    for dz in NEAR:
+    for dz in NEAR[:4]:
         cov_send(dz).start()
     hand_wait(e5, ef_s, ef_r, 3)
     chunk_add(e5, zs(3), lt, acc)
@@ -391,15 +399,16 @@
     s11, s12, s22 = curv[:128, :128], curv[:128, 128:], curv[128:, 128:]
     inv = sweep(s11, 2, times_a)
     inv = sweep(inv, 2)
-    cov_take(1)
-    cov_take(-1)
+    for dz in NEAR[:4]:
+        cov_take(dz)
+        if abs(dz) == 2:
+            cov_send(3 * dz // 2).start()
     inv_s, s12_s = split(inv), split(s12)
     w = mm3(inv_s, s12_s)
     w_s = split(w)
     inv2 = sweep(s22 - mm3(s12_s, w_s, ((0,), (0,))), 2)
-    for dz in (2, -2, 3, -3):
-        cov_take(dz)
     for d in range(2):
+        cov_take(3 - 6 * d)
         cov_onward(d).start()
     inv2 = sweep(inv2, 2)
     wq = mm3(w_s, split(inv2))
@@ -410,14 +419,11 @@
         )
     )
 
-    def back(i, _):
-        cols = pl.ds(pl.multiple_of(i * 256, 256), 256)
+    for i in range(4):
+        cols = slice(256 * i, 256 * i + 256)
         g = mm3(full_s, split(cpl[0:256, cols]))
         gv[:, cols] = g
         gh[:, cols], gl[:, cols] = split(g)
-        return 0
-
-    lax.fori_loop(0, 4, back, 0)
 
     for d in range(2):
         cov_onward(d, True).wait_recv()
@@ -434,13 +440,10 @@
             gain_copy(dx).start()
         pgr[jq] = gv[pl.ds(pl.multiple_of(32 * z + 8 * x, 8), 8), :]
 
-    def cost(i, _):
-        cols = pl.ds(pl.multiple_of(i * 256, 256), 256)
+    for i in range(4):
+        cols = slice(256 * i, 256 * i + 256)
         v = cpl[256:320, cols] - mm3(cpl_own, (gh[:, cols], gl[:, cols]))
         pcv[:, :, cols] = v.reshape(4, 16, 256)
-        return 0
-
-    lax.fori_loop(0, 4, cost, 0)
 
     def cost_copy(dx):
         return remote(pcv.at[xs(dx)], pcr.at[jq, c], cs_s.at[dx], cs_r.at[dx, c], dev(own, z, xs(dx)))
@@ -531,12 +534,13 @@
             spv[:, :, cols] = v.reshape(4, 16, 256)
 
         spread_near(half).start()
-        for dx in (1, 3):
-            spread_copy(dx, half).start()
         cols = slice(512 * half, 512 * half + 512)
         spr[x, c, :, cols] = spv[x, :, cols]
         spread_hand(0, half, c).start()
 
+    for half in range(2):
+        for dx in (1, 3):
+            spread_copy(dx, half).start()
     for half in range(2):
         spread_near(half).wait_recv()
         spread_onward(half).start()

time: 64.7 us -> 66.1 us (1.022)
  Pallas kernels: 63.9 us -> 65.2 us
    pallas_call x1, Pallas kernels: 61.6 us -> 62.9 us  [on_device(): pl.pallas_call(kernel, out_shape=(v((2, 2, 16, 1024), F32), v((2, 8, 1024...]
where the time goes in v3:
time: 66.1 us; the launch traced here: 65.9 us
  Pallas kernels  65.2 us (99%)
  between operations  0.69 us (1%)
    pallas_call x1, Pallas kernels, on_device(): pl.pallas_call(kernel, out_shape=(v((2, 2, 16, 1024), F32), v((2, 8, 1024...  62.9 us
    pallas_call x1, Pallas kernels, on_device(): pl.pallas_call(finish, out_shape=(jax.ShapeDtypeStruct((2, 2, 16, 1024),...  2.3 us

profile of v3, /device:TPU:1, one launch (start us, length us, event | category | flops | bytes accessed | tf_op | source)
XLA Modules:
  0.0 65.9 jit_solution(15070596565167873435)
XLA Ops:
  0.6 0.0 copy-start.1
  0.6 0.0 copy-start
  0.7 0.0 copy-start.2
  0.7 62.9 %shard_map.112 = (f32[2,2,16,1024]{3,2,1,0:T(8,128)S(1)}, f32[2,8,1024]{2,1,0:T(8,128)S(1)}, f32[4,2,16,1024]{3,2,1,0:T(8,128)S(1)}) custom-call(s32[8]{0:T(128)} %cw_in.1, s32[8]{0:T(128)} %po.1, f32[8,32,1024]{2,1,0:T(8,128)} %cc.1, bf16[8,4,2,16,1024]{4,3,2,1,0:T(8,128)(2,1)} %bitcast.4, bf16[8,4,2,16,256]{4,3,2,1,0:T(8,128)(2,1)} %bitcast.5, ...), custom_call_target="tpu_custom_call" | custom-call | tf_op jit(solution)/shard_map/pallas_call | solution.py:710
  63.6 0.0 copy-done.1
  63.6 0.0 copy-done
  63.6 0.0 copy-done.2
  63.6 2.3 %shard_map.113 = (f32[2,2,16,1024]{3,2,1,0:T(8,128)}, f32[2,8,1024]{2,1,0:T(8,128)}, f32[8,2,16,1024]{3,2,1,0:T(8,128)}) custom-call(s32[8]{0:T(128)S(1)} %copy-done.1, f32[2,32]{1,0:T(2,128)S(1)} %copy-done.2, f32[8,32]{1,0:T(8,128)S(1)} %copy-done, f32[2,2,16,1024]{3,2,1,0:T(8,128)S(1)} %get-tuple-element.9.pcr, f32[2,8,1024]{2,1,0:T(8,128)S(1)} %get-tuple-element.10.pgr, ...), custom_call_target="tpu_custom_call" | custom-call | tf_op jit(solution)/shard_map/pallas_call | solution.py:718
Async XLA Ops:
  0.6 63.0 %copy-start.1 = (s32[8]{0:T(128)S(1)}, s32[8]{0:T(128)}, u32[]{:S(2)}) copy-start(s32[8]{0:T(128)} %po.1) | copy-start | bytes 100
  0.6 63.0 %copy-start = (f32[8,32]{1,0:T(8,128)S(1)}, f32[8,32]{1,0:T(8,128)}, u32[]{:S(2)}) copy-start(f32[8,32]{1,0:T(8,128)} %nz.1) | copy-start | bytes 3076
  0.7 63.0 %copy-start.2 = (f32[2,32]{1,0:T(2,128)S(1)}, f32[2,32]{1,0:T(2,128)}, u32[]{:S(2)}) copy-start(f32[2,32]{1,0:T(2,128)} %sw.1) | copy-start | bytes 772

commit v4 on v3

--- a/solution.py
+++ b/solution.py
@@ -101,7 +101,7 @@
 
 ORDER = (0, 1, 3, 2)
 HOPS = ((4, 3, 3, 4), (3, 4, 4, 3))
-NEAR = (1, -1, 2, -2, 3, -3)
+NEAR = (3, -3, 2, -2, 1, -1)
 BLOCKS = 5
 
 
@@ -145,7 +145,7 @@
     for dx in range(4):
         for core in ((oc,) if dx == 0 else (c, oc)):
             pl.semaphore_signal(barrier, inc=1, device_id=dev(core, z, xs(dx)), device_id_type=MESH)
-    for dz in (1, -1, 2, -2):
+    for dz in range(1, 8):
         pl.semaphore_signal(barrier, inc=1, device_id=dev(c, zs(dz), x), device_id_type=MESH)
 
     loads = [
@@ -192,7 +192,7 @@
     lax.fori_loop(0, 4, weigh, 0)
 
     loads[3].wait()
-    pl.semaphore_wait(barrier, 11)
+    pl.semaphore_wait(barrier, 14)
 
     pair = dev(oc, z, x)
     swap = [
@@ -296,12 +296,8 @@
     e_ring = (e5, er_s, er_r, ef_s, ef_r)
 
     def cov_send(dz):
-        if abs(dz) == 3:
-            held, hop = zs(-2 * dz // 3), dz // 3
-        else:
-            held, hop = z, dz
-        part = p5.at[held, :, c]
-        return remote(part, part, pr_s.at[dz + 3], pr_r.at[dz + 3], dev(c, zs(hop), x))
+        part = p5.at[z, :, c]
+        return remote(part, part, pr_s.at[dz + 3], pr_r.at[dz + 3], dev(c, zs(dz), x))
 
     def cov_got(dz):
         part = p5.at[zs(-dz), :, c]
@@ -371,7 +367,7 @@
     ring_step(*e_ring, 4)
     cov_wait()
     cov_hand(0, c).start()
-    for dz in NEAR[:4]:
+    for dz in NEAR:
         cov_send(dz).start()
     hand_wait(e5, ef_s, ef_r, 3)
     chunk_add(e5, zs(3), lt, acc)
@@ -399,10 +395,6 @@
     s11, s12, s22 = curv[:128, :128], curv[:128, 128:], curv[128:, 128:]
     inv = sweep(s11, 2, times_a)
     inv = sweep(inv, 2)
-    for dz in NEAR[:4]:
-        cov_take(dz)
-        if abs(dz) == 2:
-            cov_send(3 * dz // 2).start()
     inv_s, s12_s = split(inv), split(s12)
     w = mm3(inv_s, s12_s)
     w_s = split(w)
@@ -411,6 +403,8 @@
         cov_take(3 - 6 * d)
         cov_onward(d).start()
     inv2 = sweep(inv2, 2)
+    for dz in NEAR[2:]:
+        cov_take(dz)
     wq = mm3(w_s, split(inv2))
     inv1 = inv + mm3(split(wq), w_s, ((1,), (1,)))
     full_s = split(
@@ -425,10 +419,6 @@
         gv[:, cols] = g
         gh[:, cols], gl[:, cols] = split(g)
 
-    for d in range(2):
-        cov_onward(d, True).wait_recv()
-        cov_far_hand(d, c).start()
-
     def gain_copy(dx):
         xx = xs(dx)
         rows = pl.ds(pl.multiple_of(32 * z + 8 * xx, 8), 8)
@@ -470,6 +460,10 @@
     @pl.when(own != c)
     def _():
         cost_copy(0).start()
+
+    for d in range(2):
+        cov_onward(d, True).wait_recv()
+        cov_far_hand(d, c).start()
 
     a_rows = a5[z, :, c].reshape(64, 1024).astype(F32)
     b_rows = b5[z, :, c].reshape(64, 256)

time: 66.1 us -> 62.7 us (0.949)
  Pallas kernels: 65.2 us -> 61.9 us
    pallas_call x1, Pallas kernels: 62.9 us -> 59.6 us  [on_device(): pl.pallas_call(kernel, out_shape=(v((2, 2, 16, 1024), F32), v((2, 8, 1024...]
where the time goes in v4:
time: 62.7 us; the launch traced here: 62.6 us
  Pallas kernels  61.9 us (99%)
  between operations  0.69 us (1%)
    pallas_call x1, Pallas kernels, on_device(): pl.pallas_call(kernel, out_shape=(v((2, 2, 16, 1024), F32), v((2, 8, 1024...  59.6 us
    pallas_call x1, Pallas kernels, on_device(): pl.pallas_call(finish, out_shape=(jax.ShapeDtypeStruct((2, 2, 16, 1024),...  2.3 us

profile of v4, /device:TPU:1, one launch (start us, length us, event | category | flops | bytes accessed | tf_op | source)
XLA Modules:
  0.0 62.6 jit_solution(3198777745385274858)
XLA Ops:
  0.6 0.0 copy-start.1
  0.6 0.0 copy-start
  0.7 0.0 copy-start.2
  0.7 59.6 %shard_map.112 = (f32[2,2,16,1024]{3,2,1,0:T(8,128)S(1)}, f32[2,8,1024]{2,1,0:T(8,128)S(1)}, f32[4,2,16,1024]{3,2,1,0:T(8,128)S(1)}) custom-call(s32[8]{0:T(128)} %cw_in.1, s32[8]{0:T(128)} %po.1, f32[8,32,1024]{2,1,0:T(8,128)} %cc.1, bf16[8,4,2,16,1024]{4,3,2,1,0:T(8,128)(2,1)} %bitcast.4, bf16[8,4,2,16,256]{4,3,2,1,0:T(8,128)(2,1)} %bitcast.5, ...), custom_call_target="tpu_custom_call" | custom-call | tf_op jit(solution)/shard_map/pallas_call | solution.py:704
  60.2 0.0 copy-done.1
  60.3 0.0 copy-done
  60.3 0.0 copy-done.2
  60.3 2.3 %shard_map.113 = (f32[2,2,16,1024]{3,2,1,0:T(8,128)}, f32[2,8,1024]{2,1,0:T(8,128)}, f32[8,2,16,1024]{3,2,1,0:T(8,128)}) custom-call(s32[8]{0:T(128)S(1)} %copy-done.1, f32[2,32]{1,0:T(2,128)S(1)} %copy-done.2, f32[8,32]{1,0:T(8,128)S(1)} %copy-done, f32[2,2,16,1024]{3,2,1,0:T(8,128)S(1)} %get-tuple-element.9.pcr, f32[2,8,1024]{2,1,0:T(8,128)S(1)} %get-tuple-element.10.pgr, ...), custom_call_target="tpu_custom_call" | custom-call | tf_op jit(solution)/shard_map/pallas_call | solution.py:712
Async XLA Ops:
  0.6 59.6 %copy-start.1 = (s32[8]{0:T(128)S(1)}, s32[8]{0:T(128)}, u32[]{:S(2)}) copy-start(s32[8]{0:T(128)} %po.1) | copy-start | bytes 100
  0.6 59.6 %copy-start = (f32[8,32]{1,0:T(8,128)S(1)}, f32[8,32]{1,0:T(8,128)}, u32[]{:S(2)}) copy-start(f32[8,32]{1,0:T(8,128)} %nz.1) | copy-start | bytes 3076
  0.7 59.6 %copy-start.2 = (f32[2,32]{1,0:T(2,128)S(1)}, f32[2,32]{1,0:T(2,128)}, u32[]{:S(2)}) copy-start(f32[2,32]{1,0:T(2,128)} %sw.1) | copy-start | bytes 772
